TPU v7x, 256 devices: a whole 4x4x8 slice. The times are simulated.
256 devices in a mesh: lat: 32 (over z_lo, y, core), ha: 8 (over x, z_hi).
Axes of the slice: x: 4, y: 4, z: 8 (z_hi: 2, z_lo: 4; z = z_hi * 4 + z_lo), core: 2. Of those that a mesh axis runs over, the one named last changes fastest.
Arguments:
- adjoint_e: float32 [3, 32, 2048, 128], P(None, 'ha', 'lat'), may hold values from -6 to 6
- adjoint_h: float32 [3, 32, 2048, 128], P(None, 'ha', 'lat'), may hold values from -6 to 6
- saved_e: bfloat16 [2, 3, 32, 2048, 128], P(None, None, 'ha', 'lat'), may hold values from -5 to 5
- labels: int32 [32, 2048, 128], P('ha', 'lat'), may hold values from 0 to 3
- eps_table: float32 [4], replicated, may hold values from 1 to 12
- chi_table: float32 [4], replicated, may hold values from 0.05 to 0.5
- density: float32 [2048, 128], P('lat'), may hold values from 0 to 1
- mon_cells: int32 [131072], P(('lat', 'ha')), may hold values from 0 to 32767
- mon_weight: float32 [131072], P(('lat', 'ha')), may hold values from 0.25 to 6.75
Outputs:
- final_e: float32 [3, 32, 2048, 128], P(None, 'ha', 'lat')
- final_h: float32 [3, 32, 2048, 128], P(None, 'ha', 'lat')
- design_grad: float32 [2048, 128], P('lat')
Inputs may be any that keep to these rules, and one draw needn't show every extreme that they name: `labels`: label 0 marks design cells. `mon_cells`: entry m names a cell of the block of block number m // 512 (lat major, ha minor), numbered in z, x, y order within the block; entries may repeat.
All inputs are finite; a program needn't handle non-finite values.
Results may differ from a plain program's by a relative error of at most 0.0003.
Values sent between devices are 32-bit elements; how exact they have to be, the bound alone decides.
No kernel may reach another device: no remote copies, remote signals or barrier semaphores. Data moves between devices by JAX's collectives and lax.ppermute only.
A program may use at most 64 MiB of HBM per device.

v0:
```python
import jax
import jax.numpy as jnp
from jax import lax
from jax.sharding import PartitionSpec as P

RADIUS = 16


sharpness = 8.0
threshold = 0.5
time_step = 0.5
epsilon = 1e-05


def passed_along(value, axis, steps):
    count = lax.axis_size(axis)
    first, last = (max(0, -steps), min(count, count - steps))
    return lax.ppermute(value, axis, [(source, source + steps) for source in range(first, last)])


def extended(cells, sides, width):
    for axis, dim in sides:
        count = lax.axis_size(axis)
        ends = count - 1
        head = lax.slice_in_dim(cells, 0, width, axis=dim)
        tail = lax.slice_in_dim(cells, cells.shape[dim] - width, cells.shape[dim], axis=dim)
        cells = jnp.concatenate(
            [
                lax.ppermute(tail, axis, [(i, (i + 1) % count) for i in range(ends)]),
                cells,
                lax.ppermute(head, axis, [((i + 1) % count, i) for i in range(ends)]),
            ],
            axis=dim,
        )
    return cells


def below_height(field, plane):
    return jnp.concatenate([plane[None], field[:-1]], 0)


def below_side(field, plane):
    return jnp.concatenate([plane[:, None], field[:, :-1]], 1)


def below_across(field):
    return jnp.concatenate([jnp.zeros_like(field[:, :, :1]), field[:, :, :-1]], 2)


def above_height(field, plane):
    return jnp.concatenate([field[1:], plane[None]], 0)


def above_side(field, plane):
    return jnp.concatenate([field[:, 1:], plane[:, None]], 1)


def above_across(field):
    return jnp.concatenate([field[:, :, 1:], jnp.zeros_like(field[:, :, :1])], 2)


def lower_planes(scaled):
    height_send = scaled[:, -1]
    side_send = scaled[:, :, -1]
    height_recv = passed_along(height_send, "ha", 1)
    side_recv = passed_along(side_send, "lat", 1)
    result = (height_recv[0:2], side_recv[1:3])
    return result


def upper_planes(field):
    height_send = field[:, 0]
    side_send = field[:, :, 0]
    height_recv = passed_along(height_send, "ha", -1)
    side_recv = passed_along(side_send, "lat", -1)
    result = (height_recv[0:2], side_recv[1:3])
    return result


def curl_lower(scaled):
    height_plane, side_plane = lower_planes(scaled)
    field_x, field_y, field_z = (scaled[0], scaled[1], scaled[2])
    curl_x = field_z - below_across(field_z) - (field_y - below_height(field_y, height_plane[1]))
    curl_y = (
        field_x
        - below_height(field_x, height_plane[0])
        - (field_z - below_side(field_z, side_plane[1]))
    )
    curl_z = field_y - below_side(field_y, side_plane[0]) - (field_x - below_across(field_x))
    return jnp.stack([curl_x, curl_y, curl_z])


def curl_upper(field):
    height_plane, side_plane = upper_planes(field)
    field_x, field_y, field_z = (field[0], field[1], field[2])
    curl_x = above_across(field_z) - field_z - (above_height(field_y, height_plane[1]) - field_y)
    curl_y = (
        above_height(field_x, height_plane[0])
        - field_x
        - (above_side(field_z, side_plane[1]) - field_z)
    )
    curl_z = above_side(field_y, side_plane[0]) - field_y - (above_across(field_x) - field_x)
    return jnp.stack([curl_x, curl_y, curl_z])


def cone(offset):
    return jnp.maximum(RADIUS + 1 - jnp.abs(offset), 0).astype(jnp.float32) / (RADIUS + 1) ** 2


def filter_rows(padded, rows):
    col_index = jnp.arange(padded.shape[1])
    across = cone(col_index[:, None] - col_index[None, :])
    smoothed = jnp.dot(
        padded, across, precision=lax.Precision.HIGHEST, preferred_element_type=jnp.float32
    )
    row_out = jnp.arange(rows)
    row_in = jnp.arange(rows + 2 * RADIUS)
    downward = cone(row_in[None, :] - RADIUS - row_out[:, None])
    return jnp.dot(
        downward, smoothed, precision=lax.Precision.HIGHEST, preferred_element_type=jnp.float32
    )


def body(
    adjoint_e, adjoint_h, saved_e, labels, eps_table, chi_table, density, mon_cells, mon_weight
):
    eps_cell = jnp.zeros(labels.shape, jnp.float32)
    chi_cell = jnp.zeros(labels.shape, jnp.float32)
    for region in range(eps_table.shape[0]):
        member = (labels == region).astype(jnp.float32)
        eps_cell = eps_cell + member * eps_table[region]
        chi_cell = chi_cell + member * chi_table[region]
    design = (labels == 0).astype(jnp.float32)
    count_all = mon_cells.shape[0] * lax.axis_size("lat") * lax.axis_size("ha")
    steps_total = saved_e.shape[0]
    shape = adjoint_e.shape
    lam_e = adjoint_e
    lam_h = adjoint_h
    plane = jnp.zeros((shape[2], shape[3]), jnp.float32)
    for index in reversed(range(steps_total)):
        forward = saved_e[index].astype(jnp.float32)
        jacobian = eps_cell[None] + 3.0 * chi_cell[None] * forward * forward
        picked = saved_e[index].reshape(3, -1)[:, mon_cells].astype(jnp.float32)
        term = jnp.sum(mon_weight * jnp.sum(picked * picked, 0))
        power = lax.psum(term, ("lat", "ha")) / count_all + epsilon
        lam_e = (
            lam_e.reshape(3, -1).at[:, mon_cells].add(mon_weight * picked / power).reshape(shape)
        )
        scaled = lam_e / jacobian
        plane = plane + jnp.sum(design * jnp.sum(scaled * forward, 0), 0)
        lam_h = lam_h - time_step * curl_lower(scaled)
        lam_e = lam_e + time_step * curl_upper(lam_h)
    extruded = lax.psum(plane, "ha")
    rows = density.shape[0]
    padded_density = extended(density, (("lat", 0),), RADIUS)
    filtered = filter_rows(padded_density, rows)
    slope = jnp.tanh(sharpness * (filtered - threshold))
    derivative = (
        sharpness
        * (1.0 - slope * slope)
        / (jnp.tanh(sharpness * threshold) + jnp.tanh(sharpness * (1.0 - threshold)))
    )
    product = derivative * extruded
    padded_product = extended(product, (("lat", 0),), RADIUS)
    return (lam_e, lam_h, filter_rows(padded_product, rows))


def solution(mesh):
    return jax.shard_map(
        body,
        mesh=mesh,
        in_specs=(
            P(None, "ha", "lat", None),
            P(None, "ha", "lat", None),
            P(None, None, "ha", "lat", None),
            P("ha", "lat", None),
            P(),
            P(),
            P("lat", None),
            P(("lat", "ha")),
            P(("lat", "ha")),
        ),
        out_specs=(P(None, "ha", "lat", None), P(None, "ha", "lat", None), P("lat", None)),
        check_vma=False,
    )
```

profile of v0, /device:TPU:38, one launch (start us, length us, event | category | flops | bytes accessed | tf_op | source)
XLA Modules:
  0.0 316.7 jit_solution(16833053180693213808)
XLA Ops:
  2.5 5.8 %copy.104 = bf16[3,32768]{0,1:T(8,128)(2,1)} copy(bf16[3,32768]{1,0:T(4,128)(2,1)S(1)} %reshape_squeeze.6) | data formatting | bytes 393216 | tf_op jit(solution)/shard_map/reshape;squeeze | solution.py:143
  8.3 5.5 %gather_fusion = bf16[512,3]{1,0:T(8,128)(2,1)S(1)} fusion(bf16[3,32768]{0,1:T(8,128)(2,1)} %copy.104, s32[1024]{0:T(1024)S(1)} %pad_clamp_fusion), kind=kCustom, calls=%fused_computation | custom fusion | bytes 8192 | tf_op jit(solution)/shard_map/gather | solution.py:143
  14.0 5.8 %copy.115 = bf16[3,32768]{0,1:T(8,128)(2,1)} copy(bf16[3,32768]{1,0:T(4,128)(2,1)S(1)} %reshape_squeeze.7) | data formatting | bytes 393216 | tf_op jit(solution)/shard_map/reshape;squeeze | solution.py:143
  19.8 5.5 %gather_fusion.1 = bf16[512,3]{1,0:T(8,128)(2,1)S(1)} fusion(bf16[3,32768]{0,1:T(8,128)(2,1)} %copy.115, s32[1024]{0:T(1024)S(1)} %pad_clamp_fusion), kind=kCustom, calls=%fused_computation.1 | custom fusion | bytes 8192 | tf_op jit(solution)/shard_map/gather | solution.py:143
  26.1 77.8 %all-reduce.8 = (f32[]{:T(128)}, f32[]{:T(128)}) all-reduce(f32[]{:T(128)} %get-tuple-element.14, f32[]{:T(128)} %get-tuple-element.13), channel_id=1, replica_groups=mesh['lat'=32,'ha'=8] {'lat','ha'}, use_global_device_ids=true, to_apply=%region_2.0 | all-reduce | flops 2 | bytes 16 | tf_op jit(solution)/shard_map/psum | solution.py:145
  105.4 8.6 %copy.103 = f32[3,4,64,128]{0,3,2,1:T(8,128)} copy(f32[3,4,64,128]{3,2,1,0:T(8,128)S(1)} %copy-done.5) | data formatting | bytes 786432 | tf_op args[0]
  114.0 14.5 %scatter_fusion = f32[3,32768]{0,1:T(8,128)} fusion(f32[3,32768]{0,1:T(8,128)} %bitcast.173, s32[512]{0:T(512)S(1)} %compare_select_fusion, f32[512,3]{1,0:T(8,128)S(1)} %copy.106), kind=kCustom, calls=%fused_computation.2 | custom fusion | flops 1536 | bytes 20480 | tf_op jit(solution)/shard_map/scatter-add | solution.py:147
  128.5 10.0 %copy.128 = f32[3,4,64,128]{3,2,1,0:T(8,128)S(1)} copy(f32[3,4,64,128]{0,3,2,1:T(8,128)} %bitcast.174) | data formatting | bytes 786432 | tf_op jit(solution)/shard_map/reshape | solution.py:147
  145.3 5.5 %collective-permute-start = (f32[3,64,128]{2,1,0:T(8,128)S(1)}, f32[3,64,128]{2,1,0:T(8,128)S(1)}, u32[]{:S(2)}, u32[]{:S(2)}) collective-permute-start(f32[3,64,128]{2,1,0:T(8,128)S(1)} %slice_bitcast_fusion.23), channel_id=1, source_target_pairs={{0,1},{1,2},{2,3},{3,4},{4,5},{5,6},{6,7},{8,9},{9,10},{10,11},{11... | collective-permute-start | bytes 294920 | tf_op jit(solution)/shard_map/ppermute | solution.py:18
  152.8 3.3 %collective-permute-start.8 = (f32[16,128]{1,0:T(8,128)S(1)}, f32[16,128]{1,0:T(8,128)S(1)}, u32[]{:S(2)}, u32[]{:S(2)}) collective-permute-start(f32[16,128]{1,0:T(8,128)S(1)} %get-tuple-element.62), channel_id=1, source_target_pairs={{0,8},{8,16},{16,24},{24,32},{32,40},{40,48},{48,56},{56,64},{64,7... | collective-permute-start | bytes 24584 | tf_op jit(solution)/shard_map/ppermute | solution.py:29
  156.1 4.4 %collective-permute-start.9 = (f32[16,128]{1,0:T(8,128)S(1)}, f32[16,128]{1,0:T(8,128)S(1)}, u32[]{:S(2)}, u32[]{:S(2)}) collective-permute-start(f32[16,128]{1,0:T(8,128)S(1)} %get-tuple-element.63), channel_id=1, source_target_pairs={{8,0},{16,8},{24,16},{32,24},{40,32},{48,40},{56,48},{64,56},{72,6... | collective-permute-start | bytes 24584 | tf_op jit(solution)/shard_map/ppermute | solution.py:31
  160.5 9.5 %copy.114 = f32[3,32768]{1,0:T(4,128)S(1)} copy(f32[3,32768]{0,1:T(8,128)} %scatter_fusion) | data formatting | bytes 786432 | tf_op jit(solution)/shard_map/scatter-add | solution.py:147
  174.6 5.4 %collective-permute-start.2 = (f32[3,64,128]{2,1,0:T(8,128)S(1)}, f32[3,64,128]{2,1,0:T(8,128)S(1)}, u32[]{:S(2)}, u32[]{:S(2)}) collective-permute-start(f32[3,64,128]{2,1,0:T(8,128)S(1)} %slice_bitcast_fusion.20), channel_id=1, source_target_pairs={{1,0},{2,1},{3,2},{4,3},{5,4},{6,5},{7,6},{9,8},{10,9},{11,10},{12... | collective-permute-start | bytes 294920 | tf_op jit(solution)/shard_map/ppermute | solution.py:18
  180.0 6.9 %collective-permute-done.2 = f32[3,64,128]{2,1,0:T(8,128)S(1)} collective-permute-done((f32[3,64,128]{2,1,0:T(8,128)S(1)}, f32[3,64,128]{2,1,0:T(8,128)S(1)}, u32[]{:S(2)}, u32[]{:S(2)}) %collective-permute-start.2) | collective-permute-done | bytes 98336 | tf_op jit(solution)/shard_map/ppermute | solution.py:18
  187.6 8.5 %copy.117 = f32[3,32768]{0,1:T(8,128)} copy(f32[3,32768]{1,0:T(4,128)S(1)} %fusion.12) | data formatting | bytes 786432 | tf_op jit(solution)/shard_map/add | solution.py:152
  196.2 14.9 %scatter_fusion.1 = f32[3,32768]{0,1:T(8,128)} fusion(f32[3,32768]{0,1:T(8,128)} %copy.117, s32[512]{0:T(512)S(1)} %compare_select_fusion, f32[512,3]{1,0:T(8,128)} %copy.118), kind=kCustom, calls=%fused_computation.3 | custom fusion | flops 1536 | bytes 20480 | tf_op jit(solution)/shard_map/scatter-add | solution.py:147
  211.0 9.5 %copy.127 = f32[3,32768]{1,0:T(4,128)S(1)} copy(f32[3,32768]{0,1:T(8,128)} %scatter_fusion.1) | data formatting | bytes 786432 | tf_op jit(solution)/shard_map/scatter-add | solution.py:147
  220.5 10.0 %copy.129 = f32[3,4,64,128]{3,2,1,0:T(8,128)S(1)} copy(f32[3,4,64,128]{0,3,2,1:T(8,128)} %bitcast.172) | data formatting | bytes 786432 | tf_op jit(solution)/shard_map/reshape | solution.py:147
  233.2 47.5 %psum.23 = f32[64,128]{1,0:T(8,128)S(1)} all-reduce(f32[64,128]{1,0:T(8,128)S(1)} %add.115), channel_id=1, replica_groups=mesh['lat'=32,'ha'=8] {'ha'}, use_global_device_ids=true, to_apply=%region_12.0 | all-reduce | flops 8192 | bytes 65536 | tf_op jit(solution)/shard_map/psum | solution.py:153
  283.6 4.4 %collective-permute-start.4 = (f32[3,64,128]{2,1,0:T(8,128)}, f32[3,64,128]{2,1,0:T(8,128)S(1)}, u32[]{:S(2)}, u32[]{:S(2)}) collective-permute-start(f32[3,64,128]{2,1,0:T(8,128)} %slice_bitcast_fusion.19), channel_id=1, source_target_pairs={{0,1},{1,2},{2,3},{3,4},{4,5},{5,6},{6,7},{8,9},{9,10},{10,11},{11... | collective-permute-start | bytes 294920 | tf_op jit(solution)/shard_map/ppermute | solution.py:18
  289.9 5.8 %collective-permute-start.11 = (f32[16,128]{1,0:T(8,128)S(1)}, f32[16,128]{1,0:T(8,128)S(1)}, u32[]{:S(2)}, u32[]{:S(2)}) collective-permute-start(f32[16,128]{1,0:T(8,128)S(1)} %get-tuple-element.61), channel_id=1, source_target_pairs={{8,0},{16,8},{24,16},{32,24},{40,32},{48,40},{56,48},{64,56},{72,6... | collective-permute-start | bytes 24584 | tf_op jit(solution)/shard_map/ppermute | solution.py:31
  299.4 5.7 %collective-permute-start.7 = (f32[3,4,128]{2,1,0:T(4,128)S(1)}, f32[3,4,128]{2,1,0:T(4,128)S(1)}, u32[]{:S(2)}, u32[]{:S(2)}) collective-permute-start(f32[3,4,128]{2,1,0:T(4,128)S(1)} %bitcast.199), channel_id=1, source_target_pairs={{8,0},{16,8},{24,16},{32,24},{40,32},{48,40},{56,48},{64,56},{72,6... | collective-permute-start | bytes 18440 | tf_op jit(solution)/shard_map/ppermute | solution.py:18
  305.2 6.3 %collective-permute-start.6 = (f32[3,64,128]{2,1,0:T(8,128)S(1)}, f32[3,64,128]{2,1,0:T(8,128)S(1)}, u32[]{:S(2)}, u32[]{:S(2)}) collective-permute-start(f32[3,64,128]{2,1,0:T(8,128)S(1)} %slice_bitcast_fusion.16), channel_id=1, source_target_pairs={{1,0},{2,1},{3,2},{4,3},{5,4},{6,5},{7,6},{9,8},{10,9},{11,10},{12... | collective-permute-start | bytes 294920 | tf_op jit(solution)/shard_map/ppermute | solution.py:18
  311.5 4.1 %collective-permute-done.6 = f32[3,64,128]{2,1,0:T(8,128)S(1)} collective-permute-done((f32[3,64,128]{2,1,0:T(8,128)S(1)}, f32[3,64,128]{2,1,0:T(8,128)S(1)}, u32[]{:S(2)}, u32[]{:S(2)}) %collective-permute-start.6) | collective-permute-done | bytes 98336 | tf_op jit(solution)/shard_map/ppermute | solution.py:18
  (112 shorter events, 29.0 us)
Async XLA Ops:
  0.6 24.8 %copy-start.8 = (f32[512]{0:T(512)S(1)}, f32[512]{0:T(512)}, u32[]{:S(2)}) copy-start(f32[512]{0:T(512)} %param.17) | copy-start | bytes 6148
  0.6 104.7 %copy-start.5 = (f32[3,4,64,128]{3,2,1,0:T(8,128)S(1)}, f32[3,4,64,128]{3,2,1,0:T(8,128)}, u32[]{:S(2)}) copy-start(f32[3,4,64,128]{3,2,1,0:T(8,128)} %param.9) | copy-start | bytes 1179652
  105.4 33.2 %copy-start.10 = (f32[4]{0:T(128)S(1)}, f32[4]{0:T(128)}, u32[]{:S(2)}) copy-start(f32[4]{0:T(128)} %param.13) | copy-start | bytes 52
  105.4 33.9 %copy-start.11 = (f32[4]{0:T(128)S(1)}, f32[4]{0:T(128)}, u32[]{:S(2)}) copy-start(f32[4]{0:T(128)} %param.14) | copy-start | bytes 52
  105.4 34.5 %copy-start.7 = (s32[4,64,128]{2,1,0:T(8,128)S(1)}, s32[4,64,128]{2,1,0:T(8,128)}, u32[]{:S(2)}) copy-start(s32[4,64,128]{2,1,0:T(8,128)} %param.12) | copy-start | bytes 393220
  105.4 39.8 %copy-start.1 = (bf16[2,3,4,64,128]{4,3,2,1,0:T(8,128)(2,1)S(1)}, bf16[2,3,4,64,128]{4,3,2,1,0:T(8,128)(2,1)}, u32[]{:S(2)}) copy-start(bf16[2,3,4,64,128]{4,3,2,1,0:T(8,128)(2,1)} %param.11) | copy-start | bytes 1179652
  105.4 47.3 %copy-start.9 = (f32[64,128]{1,0:T(8,128)S(1)}, f32[64,128]{1,0:T(8,128)}, u32[]{:S(2)}) copy-start(f32[64,128]{1,0:T(8,128)} %param.15) | copy-start | bytes 98308
  128.5 43.4 %copy-start.2 = (f32[3,4,64,128]{3,2,1,0:T(8,128)S(1)}, f32[3,4,64,128]{3,2,1,0:T(8,128)}, u32[]{:S(2)}) copy-start(f32[3,4,64,128]{3,2,1,0:T(8,128)} %param.10) | copy-start | bytes 1179652
  142.6 17.9 %copy-start.6 = (pred[4,64,128]{2,1,0:T(8,128)(4,1)}, pred[4,64,128]{2,1,0:T(8,128)(4,1)S(1)}, u32[]{:S(2)}) copy-start(pred[4,64,128]{2,1,0:T(8,128)(4,1)S(1)} %get-tuple-element.18) | copy-start | bytes 98308
  145.3 26.4 %collective-permute-start = (f32[3,64,128]{2,1,0:T(8,128)S(1)}, f32[3,64,128]{2,1,0:T(8,128)S(1)}, u32[]{:S(2)}, u32[]{:S(2)}) collective-permute-start(f32[3,64,128]{2,1,0:T(8,128)S(1)} %slice_bitcast_fusion.23), channel_id=1, source_target_pairs={{0,1},{1,2},{2,3},{3,4},{4,5},{5,6},{6,7},{8,9},{9,10},{10,11},{11... | collective-permute-start | bytes 294920 | tf_op jit(solution)/shard_map/ppermute | solution.py:18
  150.8 20.1 %collective-permute-start.1 = (f32[3,4,128]{2,1,0:T(4,128)S(1)}, f32[3,4,128]{2,1,0:T(4,128)S(1)}, u32[]{:S(2)}, u32[]{:S(2)}) collective-permute-start(f32[3,4,128]{2,1,0:T(4,128)S(1)} %bitcast.197), channel_id=1, source_target_pairs={{0,8},{8,16},{16,24},{24,32},{32,40},{40,48},{48,56},{56,64},{64,7... | collective-permute-start | bytes 18440 | tf_op jit(solution)/shard_map/ppermute | solution.py:18
  152.8 18.1 %collective-permute-start.8 = (f32[16,128]{1,0:T(8,128)S(1)}, f32[16,128]{1,0:T(8,128)S(1)}, u32[]{:S(2)}, u32[]{:S(2)}) collective-permute-start(f32[16,128]{1,0:T(8,128)S(1)} %get-tuple-element.62), channel_id=1, source_target_pairs={{0,8},{8,16},{16,24},{24,32},{32,40},{40,48},{48,56},{56,64},{64,7... | collective-permute-start | bytes 24584 | tf_op jit(solution)/shard_map/ppermute | solution.py:29
  156.1 14.8 %collective-permute-start.9 = (f32[16,128]{1,0:T(8,128)S(1)}, f32[16,128]{1,0:T(8,128)S(1)}, u32[]{:S(2)}, u32[]{:S(2)}) collective-permute-start(f32[16,128]{1,0:T(8,128)S(1)} %get-tuple-element.63), channel_id=1, source_target_pairs={{8,0},{16,8},{24,16},{32,24},{40,32},{48,40},{56,48},{64,56},{72,6... | collective-permute-start | bytes 24584 | tf_op jit(solution)/shard_map/ppermute | solution.py:31
  171.8 48.7 %copy-start.4 = (f32[1,4,64,128]{3,2,1,0:T(8,128)}, f32[1,4,64,128]{3,2,1,0:T(8,128)S(1)}, u32[]{:S(2)}) copy-start(f32[1,4,64,128]{3,2,1,0:T(8,128)S(1)} %get-tuple-element.47) | copy-start | bytes 393220
  171.9 48.6 %copy-start.3 = (f32[1,4,64,128]{3,2,1,0:T(8,128)}, f32[1,4,64,128]{3,2,1,0:T(8,128)S(1)}, u32[]{:S(2)}) copy-start(f32[1,4,64,128]{3,2,1,0:T(8,128)S(1)} %get-tuple-element.44) | copy-start | bytes 393220
  172.1 7.9 %collective-permute-start.3 = (f32[3,4,128]{2,1,0:T(4,128)S(1)}, f32[3,4,128]{2,1,0:T(4,128)S(1)}, u32[]{:S(2)}, u32[]{:S(2)}) collective-permute-start(f32[3,4,128]{2,1,0:T(4,128)S(1)} %bitcast.198), channel_id=1, source_target_pairs={{8,0},{16,8},{24,16},{32,24},{40,32},{48,40},{56,48},{64,56},{72,6... | collective-permute-start | bytes 18440 | tf_op jit(solution)/shard_map/ppermute | solution.py:18
  174.6 12.3 %collective-permute-start.2 = (f32[3,64,128]{2,1,0:T(8,128)S(1)}, f32[3,64,128]{2,1,0:T(8,128)S(1)}, u32[]{:S(2)}, u32[]{:S(2)}) collective-permute-start(f32[3,64,128]{2,1,0:T(8,128)S(1)} %slice_bitcast_fusion.20), channel_id=1, source_target_pairs={{1,0},{2,1},{3,2},{4,3},{5,4},{6,5},{7,6},{9,8},{10,9},{11,10},{12... | collective-permute-start | bytes 294920 | tf_op jit(solution)/shard_map/ppermute | solution.py:18
  281.6 14.1 %collective-permute-start.10 = (f32[16,128]{1,0:T(8,128)S(1)}, f32[16,128]{1,0:T(8,128)S(1)}, u32[]{:S(2)}, u32[]{:S(2)}) collective-permute-start(f32[16,128]{1,0:T(8,128)S(1)} %get-tuple-element.60), channel_id=1, source_target_pairs={{0,8},{8,16},{16,24},{24,32},{32,40},{40,48},{48,56},{56,64},{64,7... | collective-permute-start | bytes 24584 | tf_op jit(solution)/shard_map/ppermute | solution.py:29
  283.6 14.5 %collective-permute-start.4 = (f32[3,64,128]{2,1,0:T(8,128)}, f32[3,64,128]{2,1,0:T(8,128)S(1)}, u32[]{:S(2)}, u32[]{:S(2)}) collective-permute-start(f32[3,64,128]{2,1,0:T(8,128)} %slice_bitcast_fusion.19), channel_id=1, source_target_pairs={{0,1},{1,2},{2,3},{3,4},{4,5},{5,6},{6,7},{8,9},{9,10},{10,11},{11... | collective-permute-start | bytes 294920 | tf_op jit(solution)/shard_map/ppermute | solution.py:18
  288.0 7.7 %collective-permute-start.5 = (f32[3,4,128]{2,1,0:T(4,128)S(1)}, f32[3,4,128]{2,1,0:T(4,128)S(1)}, u32[]{:S(2)}, u32[]{:S(2)}) collective-permute-start(f32[3,4,128]{2,1,0:T(4,128)S(1)} %bitcast.196), channel_id=1, source_target_pairs={{0,8},{8,16},{16,24},{24,32},{32,40},{40,48},{48,56},{56,64},{64,7... | collective-permute-start | bytes 18440 | tf_op jit(solution)/shard_map/ppermute | solution.py:18
  289.9 7.1 %collective-permute-start.11 = (f32[16,128]{1,0:T(8,128)S(1)}, f32[16,128]{1,0:T(8,128)S(1)}, u32[]{:S(2)}, u32[]{:S(2)}) collective-permute-start(f32[16,128]{1,0:T(8,128)S(1)} %get-tuple-element.61), channel_id=1, source_target_pairs={{8,0},{16,8},{24,16},{32,24},{40,32},{48,40},{56,48},{64,56},{72,6... | collective-permute-start | bytes 24584 | tf_op jit(solution)/shard_map/ppermute | solution.py:31
  299.3 17.4 %copy-start = (f32[3,4,64,128]{3,2,1,0:T(8,128)}, f32[3,4,64,128]{3,2,1,0:T(8,128)S(1)}, u32[]{:S(2)}) copy-start(f32[3,4,64,128]{3,2,1,0:T(8,128)S(1)} %fusion.18) | copy-start | bytes 1179652
  299.4 12.1 %collective-permute-start.7 = (f32[3,4,128]{2,1,0:T(4,128)S(1)}, f32[3,4,128]{2,1,0:T(4,128)S(1)}, u32[]{:S(2)}, u32[]{:S(2)}) collective-permute-start(f32[3,4,128]{2,1,0:T(4,128)S(1)} %bitcast.199), channel_id=1, source_target_pairs={{8,0},{16,8},{24,16},{32,24},{40,32},{48,40},{56,48},{64,56},{72,6... | collective-permute-start | bytes 18440 | tf_op jit(solution)/shard_map/ppermute | solution.py:18
  305.2 10.4 %collective-permute-start.6 = (f32[3,64,128]{2,1,0:T(8,128)S(1)}, f32[3,64,128]{2,1,0:T(8,128)S(1)}, u32[]{:S(2)}, u32[]{:S(2)}) collective-permute-start(f32[3,64,128]{2,1,0:T(8,128)S(1)} %slice_bitcast_fusion.16), channel_id=1, source_target_pairs={{1,0},{2,1},{3,2},{4,3},{5,4},{6,5},{7,6},{9,8},{10,9},{11,10},{12... | collective-permute-start | bytes 294920 | tf_op jit(solution)/shard_map/ppermute | solution.py:18
where the time goes:
time: 320 us; the launch traced here: 317 us
  blocking collectives  125 us (39%)
  local copies, waits for them, and re-layouts  83.7 us (26%)
  starting transfers between devices  48.8 us (15%)
  other arithmetic  41 us (13%)
  waiting for transfers between devices  12.4 us (4%)
    psum x1, blocking collectives, body(): power = lax.psum(term, ('lat', 'ha')) / count_all + epsilon  77.8 us
    psum x1, blocking collectives, body(): extruded = lax.psum(plane, 'ha')  47.5 us
    ppermute x8, starting transfers between devices, passed_along(): lax.ppermute(value, axis, [(source, source + steps) for source in range(f...  33.5 us
    scatter-add x2, other arithmetic, body(): lam_e.reshape(3, -1).at[:, mon_cells].add(mon_weight * picked / power)  29.4 us
    reshape x2, local copies, waits for them, and re-layouts, body(): lam_e.reshape(3, -1).at[:, mon_cells].add(mon_weight * picked / power)  20 us
    scatter-add x2, local copies, waits for them, and re-layouts, body(): lam_e.reshape(3, -1).at[:, mon_cells].add(mon_weight * picked / power)  18.9 us
    another operation x4, local copies, waits for them, and re-layouts, body(): picked = saved_e[index].reshape(3, -1)[:, mon_cells].astype(jnp.float32)  11.7 us
    gather x4, local copies, waits for them, and re-layouts, body(): picked = saved_e[index].reshape(3, -1)[:, mon_cells].astype(jnp.float32)  11.2 us
  transfers between devices with their start and end apart: 12, of which 3 were waited for; matrix products, arithmetic and copies ran while one was open for 4% of the time, Pallas kernels for 0%

commit v1 on v0

v1 whole, which is shorter than its diff:
```python
import jax
import jax.numpy as jnp
from jax import lax
from jax.experimental import pallas as pl
from jax.experimental.pallas import tpu as pltpu
from jax.sharding import PartitionSpec as P

RADIUS = 16
PAD = 8

sharpness = 8.0
threshold = 0.5
time_step = 0.5
epsilon = 1e-05

F32 = jnp.float32
VMEM = pl.BlockSpec(memory_space=pltpu.VMEM)
SMEM = pl.BlockSpec(memory_space=pltpu.SMEM)


def shifted(value, axis, steps):
    count = lax.axis_size(axis)
    return lax.ppermute(
        value, axis, [(i, i + steps) for i in range(count) if 0 <= i + steps < count]
    )


def lower_y(v):
    lane = lax.broadcasted_iota(jnp.int32, v.shape, 1)
    return jnp.where(lane == 0, 0.0, pltpu.roll(v, 1, 1))


def upper_y(v):
    lane = lax.broadcasted_iota(jnp.int32, v.shape, 1)
    last = v.shape[1] - 1
    return jnp.where(lane == last, 0.0, pltpu.roll(v, last, 1))


def lower_x(v):
    return pltpu.roll(v, 1, 0)


def upper_x(v):
    return pltpu.roll(v, v.shape[0] - 1, 0)


def smooth(padded, rows):
    cols = padded.shape[1]
    tall = padded.shape[0]

    def cone(offset):
        return jnp.maximum(RADIUS + 1 - jnp.abs(offset), 0).astype(F32)

    a = lax.broadcasted_iota(jnp.int32, (cols, cols), 0)
    b = lax.broadcasted_iota(jnp.int32, (cols, cols), 1)
    across = jnp.dot(
        padded, cone(a - b), precision=lax.Precision.HIGHEST, preferred_element_type=F32
    )
    r = lax.broadcasted_iota(jnp.int32, (rows, tall), 0)
    s = lax.broadcasted_iota(jnp.int32, (rows, tall), 1)
    down = jnp.dot(
        cone(s - RADIUS - r), across, precision=lax.Precision.HIGHEST, preferred_element_type=F32
    )
    return down * (1.0 / (RADIUS + 1) ** 4)


def prepare_kernel(e, h, sv, labels, density, cells, weight, w_out, power_out, nxt, prv):
    cz, cx, ny = labels.shape
    count = cells.shape[1]
    cell = cells[...]
    row = cell // ny
    col = cell % ny
    rows_hot = jnp.where(
        lax.broadcasted_iota(jnp.int32, (cz * cx, count), 0) == row, weight[...], 0.0
    )
    cols_hot = (lax.broadcasted_iota(jnp.int32, (ny, count), 0) == col).astype(F32)
    w = lax.dot_general(
        rows_hot,
        cols_hot,
        (((1,), (1,)), ((), ())),
        precision=lax.Precision.HIGHEST,
        preferred_element_type=F32,
    ).reshape(cz, cx, ny)
    w_out[...] = w
    steps = sv.shape[0]
    lane = lax.broadcasted_iota(jnp.int32, (1, ny), 1)
    packed = jnp.zeros((1, ny), F32)
    for k in range(steps):
        total = jnp.zeros((cx, ny), F32)
        for z in range(cz):
            square = jnp.zeros((cx, ny), F32)
            for c in range(3):
                f = sv[k, c, z].astype(F32)
                square = square + f * f
                slot = (1 + 2 * (steps - 1 - k)) * 3 * cz + c * cz + z
                nxt[slot] = f[cx - PAD :]
                prv[slot] = f[:PAD]
            total = total + w[z] * square
        packed = jnp.where(lane == k, jnp.sum(total), packed)
    power_out[...] = packed
    for c in range(3):
        for z in range(cz):
            nxt[c * cz + z] = e[c, z, cx - PAD :]
            prv[c * cz + z] = e[c, z, :PAD]
            nxt[(6 + c) * cz + z] = h[c, z, cx - PAD :]
            prv[(6 + c) * cz + z] = h[c, z, :PAD]
    for z in range(cz):
        nxt[12 * cz + z] = labels[z, cx - PAD :].astype(F32)
        prv[12 * cz + z] = labels[z, :PAD].astype(F32)
        nxt[13 * cz + z] = w[z, cx - PAD :]
        prv[13 * cz + z] = w[z, :PAD]
    for t in range(RADIUS // PAD):
        nxt[14 * cz + t] = density[cx - RADIUS + t * PAD : cx - RADIUS + (t + 1) * PAD]
        prv[14 * cz + t] = density[t * PAD : (t + 1) * PAD]


def region(labels, lo, hi, eps_t, chi_t, z, cz):
    lab = jnp.concatenate([lo[12 * cz + z], labels[z].astype(F32), hi[12 * cz + z]], 0)
    eps = jnp.full(lab.shape, eps_t[0], F32)
    chi = jnp.full(lab.shape, 3.0 * chi_t[0], F32)
    for r in range(1, eps_t.shape[0]):
        eps = jnp.where(lab == float(r), eps_t[r], eps)
        chi = jnp.where(lab == float(r), 3.0 * chi_t[r], chi)
    return lab, eps, chi


def source_and_lower(
    k, get_e, get_h, put_e, put_h, sv, labels, w, lo, hi, eps_t, chi_t, inv_power, s, mask_s, mask_h
):
    cz, cx, ny = labels.shape
    steps = sv.shape[0]
    base = (1 + 2 * (steps - 1 - k)) * 3 * cz
    plane = jnp.zeros((cx, ny), F32)
    for z in range(cz):
        lab, eps, chi = region(labels, lo, hi, eps_t, chi_t, z, cz)
        wz = jnp.concatenate([lo[13 * cz + z], w[z], hi[13 * cz + z]], 0) * inv_power
        along = jnp.zeros((cx, ny), F32)
        for c in range(3):
            slot = base + c * cz + z
            f = jnp.concatenate([lo[slot], sv[k, c, z].astype(F32), hi[slot]], 0)
            ec = get_e(c, z) + wz * f
            put_e(c, z, ec)
            sc = ec / (eps + chi * f * f)
            if mask_s is not None:
                sc = sc * mask_s
            s[c, z] = sc
            along = along + (sc * f)[PAD : PAD + cx]
        plane = plane + jnp.where(lab[PAD : PAD + cx] == 0.0, along, 0.0)
    for z in range(cz):
        sx, sy, sz = s[0, z], s[1, z], s[2, z]
        cx_ = sz - lower_y(sz) - sy
        cy_ = sx - sz + lower_x(sz)
        cz_ = sy - lower_x(sy) - sx + lower_y(sx)
        if z > 0:
            cx_ = cx_ + s[1, z - 1]
            cy_ = cy_ - s[0, z - 1]
        for c, curl in enumerate((cx_, cy_, cz_)):
            put_h(c, z, (get_h(c, z) - time_step * curl) * mask_h)
    return plane


def row_masks(tall, cx):
    row = lax.broadcasted_iota(jnp.int32, (tall, 128), 0)
    lat = lax.axis_index("lat")
    first = jnp.where(lat == 0, PAD, 0)
    last = jnp.where(lat == lax.axis_size("lat") - 1, PAD + cx, tall)
    mask_s = jnp.where(row >= first, 1.0, 0.0)
    mask_h = jnp.where(row < last, 1.0, 0.0)
    return mask_s, mask_h


def first_kernel(
    k, e, h, sv, labels, w, lo, hi, density, power, eps_t, chi_t, e_out, h_out, up, down, plane_out, deriv_out, s
):
    cz, cx, ny = labels.shape
    tall = e_out.shape[2]
    _, mask_h = row_masks(tall, cx)

    def get_e(c, z):
        return jnp.concatenate([lo[c * cz + z], e[c, z], hi[c * cz + z]], 0)

    def get_h(c, z):
        slot = (6 + c) * cz + z
        return jnp.concatenate([lo[slot], h[c, z], hi[slot]], 0)

    def put_e(c, z, v):
        e_out[c, z] = v

    def put_h(c, z, v):
        h_out[c, z] = v

    plane_out[...] = source_and_lower(
        k, get_e, get_h, put_e, put_h, sv, labels, w, lo, hi, eps_t, chi_t, power[k], s, None, mask_h
    )
    for c in range(2):
        up[c] = s[c, cz - 1]
        down[c] = h_out[c, 0]
    tiles = RADIUS // PAD
    padded = jnp.concatenate(
        [lo[14 * cz + t] for t in range(tiles)]
        + [density[...]]
        + [hi[14 * cz + t] for t in range(tiles)],
        0,
    )
    slope = jnp.tanh(sharpness * (smooth(padded, cx) - threshold))
    scale = jnp.tanh(jnp.full((1, ny), sharpness * threshold, F32)) + jnp.tanh(
        jnp.full((1, ny), sharpness * (1.0 - threshold), F32)
    )
    deriv_out[...] = sharpness * (1.0 - slope * slope) / scale


def finish_lower(h, get_h, recv_lo, recv_hi, up, mask_h):
    cz = h.shape[1]
    top = jnp.where(lax.axis_index("ha") == lax.axis_size("ha") - 1, 0.0, 1.0)
    low_x = h[0, 0] - time_step * (recv_lo[1] * mask_h)
    low_y = h[1, 0] + time_step * (recv_lo[0] * mask_h)
    above_x = (recv_hi[0] - time_step * up[1] * mask_h) * top
    above_y = (recv_hi[1] + time_step * up[0] * mask_h) * top
    return low_x, low_y, above_x, above_y


def upper_curl(hz_layer, above_x, above_y):
    hx, hy, hz = hz_layer
    curl_x = upper_y(hz) - hz - (above_y - hy)
    curl_y = above_x - hx - (upper_x(hz) - hz)
    curl_z = upper_x(hy) - hy - (upper_y(hx) - hx)
    return curl_x, curl_y, curl_z


def second_kernel(
    k, e, h, sv, labels, w, lo, hi, power, eps_t, chi_t, recv_lo, recv_hi, up1, plane1, deriv,
    e_out, h_out, up, down, product, s, e1,
):
    cz, cx, ny = labels.shape
    tall = e.shape[2]
    mask_s, mask_h = row_masks(tall, cx)
    low_x, low_y, above_x, above_y = finish_lower(h, None, recv_lo, recv_hi, up1, mask_h)

    def layer(c, z):
        if z == 0 and c < 2:
            return (low_x, low_y)[c]
        if z == cz:
            return (above_x, above_y)[c]
        return h[c, z]

    for z in range(cz):
        curls = upper_curl([layer(c, z) for c in range(3)], layer(0, z + 1), layer(1, z + 1))
        for c in range(3):
            e1[c, z] = e[c, z] + time_step * curls[c]

    def get_e(c, z):
        return e1[c, z]

    def put_e(c, z, v):
        e_out[c, z] = v

    def put_h(c, z, v):
        h_out[c, z] = v

    plane = source_and_lower(
        k, get_e, layer, put_e, put_h, sv, labels, w, lo, hi, eps_t, chi_t, power[k], s, mask_s, mask_h
    )
    product[...] = (plane1[...] + plane) * deriv[...]
    for c in range(2):
        up[c] = s[c, cz - 1]
        down[c] = h_out[c, 0]


def smooth_kernel(lo, mid, hi, out):
    out[...] = smooth(jnp.concatenate([lo[...], mid[...], hi[...]], 0), mid.shape[0])


def final_kernel(e, h, recv_lo, recv_hi, up, parts, e_out, h_out, grad):
    cz = h.shape[1]
    tall = e.shape[2]
    cx = e_out.shape[2]
    own = slice(PAD, PAD + cx)
    _, mask_h = row_masks(tall, cx)
    low_x, low_y, above_x, above_y = finish_lower(h, None, recv_lo, recv_hi, up, mask_h)

    def layer(c, z):
        if z == 0 and c < 2:
            return (low_x, low_y)[c]
        if z == cz:
            return (above_x, above_y)[c]
        return h[c, z]

    for z in range(cz):
        parts_h = [layer(c, z) for c in range(3)]
        curls = upper_curl(parts_h, layer(0, z + 1), layer(1, z + 1))
        for c in range(3):
            e_out[c, z] = (e[c, z] + time_step * curls[c])[own]
            h_out[c, z] = parts_h[c][own]
    total = parts[0]
    for i in range(1, parts.shape[0]):
        total = total + parts[i]
    grad[...] = total


def call(kernel, outs, specs, name, scratch=()):
    return pl.pallas_call(
        kernel,
        out_shape=[jax.ShapeDtypeStruct(o, F32) for o in outs],
        in_specs=specs,
        out_specs=[VMEM] * len(outs),
        scratch_shapes=[pltpu.VMEM(x, F32) for x in scratch],
        name=name,
    )


def body(
    adjoint_e, adjoint_h, saved_e, labels, eps_table, chi_table, density, mon_cells, mon_weight
):
    cz, cx, ny = labels.shape
    steps = saved_e.shape[0]
    tall = cx + 2 * PAD
    devices = lax.axis_size("lat") * lax.axis_size("ha")
    count_all = mon_cells.shape[0] * devices
    tiles = 14 * cz + RADIUS // PAD

    w, partial, nxt, prv = call(
        prepare_kernel,
        [(cz, cx, ny), (1, ny), (tiles, PAD, ny), (tiles, PAD, ny)],
        [VMEM] * 7,
        "prepare",
    )(
        adjoint_e,
        adjoint_h,
        saved_e,
        labels,
        density,
        mon_cells.reshape(1, -1),
        mon_weight.reshape(1, -1),
    )
    lo = shifted(nxt, "lat", 1)
    hi = shifted(prv, "lat", -1)
    spread = lax.all_to_all(
        jnp.broadcast_to(partial[None], (devices, 1, ny)), ("lat", "ha"), 0, 0
    )
    power = jnp.sum(spread, 0)[0, :steps] / count_all + epsilon
    inv_power = 1.0 / power

    field = (3, cz, tall, ny)
    edge = (2, tall, ny)
    e1, h1, up1, down1, plane1, deriv = call(
        lambda *refs: first_kernel(1, *refs),
        [field, field, edge, edge, (cx, ny), (cx, ny)],
        [VMEM] * 8 + [SMEM] * 3,
        "first",
        [field],
    )(adjoint_e, adjoint_h, saved_e, labels, w, lo, hi, density, inv_power, eps_table, chi_table)
    recv_lo = shifted(up1, "ha", 1)
    recv_hi = shifted(down1, "ha", -1)
    e0, h0, up0, down0, product = call(
        lambda *refs: second_kernel(0, *refs),
        [field, field, edge, edge, (cx, ny)],
        [VMEM] * 7 + [SMEM] * 3 + [VMEM] * 5,
        "second",
        [field, field],
    )(
        e1, h1, saved_e, labels, w, lo, hi, inv_power, eps_table, chi_table,
        recv_lo, recv_hi, up1, plane1, deriv,
    )
    below = shifted(product[cx - RADIUS :], "lat", 1)
    above = shifted(product[:RADIUS], "lat", -1)
    recv_lo = shifted(up0, "ha", 1)
    recv_hi = shifted(down0, "ha", -1)
    (local,) = call(smooth_kernel, [(cx, ny)], [VMEM] * 3, "smooth")(below, product, above)
    members = lax.axis_size("ha")
    parts = lax.all_to_all(jnp.broadcast_to(local[None], (members, cx, ny)), "ha", 0, 0)
    final_e, final_h, grad = call(
        final_kernel, [adjoint_e.shape, adjoint_h.shape, (cx, ny)], [VMEM] * 6, "final"
    )(e0, h0, recv_lo, recv_hi, up0, parts)
    return (final_e, final_h, grad)


def solution(mesh):
    return jax.shard_map(
        body,
        mesh=mesh,
        in_specs=(
            P(None, "ha", "lat", None),
            P(None, "ha", "lat", None),
            P(None, None, "ha", "lat", None),
            P("ha", "lat", None),
            P(),
            P(),
            P("lat", None),
            P(("lat", "ha")),
            P(("lat", "ha")),
        ),
        out_specs=(P(None, "ha", "lat", None), P(None, "ha", "lat", None), P("lat", None)),
        check_vma=False,
    )
```

time: 320 us -> 101 us (0.32)
  blocking collectives: 125 us -> 0 us
  local copies, waits for them, and re-layouts: 83.7 us -> 6.3 us
  other arithmetic: 41 us -> 0.63 us
  waiting for transfers between devices: 12.4 us -> 27.7 us
  Pallas kernels: 0 us -> 13 us
  starting transfers between devices: 48.8 us -> 52.3 us
    psum x2 -> x0, blocking collectives: 125 us -> none  [the longest x1 77.8 us: body(): power = lax.psum(term, ('lat', 'ha')) / count_all + epsilon]
    scatter-add x2 -> x0, other arithmetic: 29.4 us -> none  [body(): lam_e.reshape(3, -1).at[:, mon_cells].add(mon_weight * picked / power)]
    reshape x2 -> x0, local copies, waits for them, and re-layouts: 20 us -> none  [body(): lam_e.reshape(3, -1).at[:, mon_cells].add(mon_weight * picked / power)]
    all_to_all x0 -> x2, starting transfers between devices: none -> 19.3 us  [the longest x1 14.3 us: body(): lax.all_to_all(jnp.broadcast_to(partial[None], (devices, 1, ny)), ('lat',...]
    scatter-add x2 -> x0, local copies, waits for them, and re-layouts: 18.9 us -> none  [body(): lam_e.reshape(3, -1).at[:, mon_cells].add(mon_weight * picked / power)]
    ppermute x12 -> x8, starting transfers between devices: 48.8 us -> 33 us  [shifted(): lax.ppermute(value, axis, [(i, i + steps) for i in range(count) if 0 <= i...]
    pallas_call x0 -> x5, Pallas kernels: none -> 13 us  [the longest x1 3.09 us: body(): call(lambda *refs: second_kernel(0, *refs), [field, field, edge, edge, (c...]
    ppermute x12 -> x8, waiting for transfers between devices: 12.4 us -> 24.4 us  [shifted(): lax.ppermute(value, axis, [(i, i + steps) for i in range(count) if 0 <= i...]
  transfers between devices with their start and end apart: 12 -> 10, of which waited for: 3 -> 6; matrix products, arithmetic and copies ran while one was open for 4% -> 1% of each run, Pallas kernels for 0% -> 0%
where the time goes in v1:
time: 101 us
  starting transfers between devices  52.3 us (52%)
  waiting for transfers between devices  27.7 us (27%)
  Pallas kernels  13 us (13%)
  local copies, waits for them, and re-layouts  6.3 us (6%)
    ppermute x8, starting transfers between devices, shifted(): lax.ppermute(value, axis, [(i, i + steps) for i in range(count) if 0 <= i...  33 us
    ppermute x8, waiting for transfers between devices, shifted(): lax.ppermute(value, axis, [(i, i + steps) for i in range(count) if 0 <= i...  24.4 us
    all_to_all x1, starting transfers between devices, body(): lax.all_to_all(jnp.broadcast_to(partial[None], (devices, 1, ny)), ('lat',...  14.3 us
    all_to_all x1, starting transfers between devices, body(): lax.all_to_all(jnp.broadcast_to(local[None], (members, cx, ny)), 'ha', 0, 0)  4.95 us
    unnamed x26, local copies, waits for them, and re-layouts  3.39 us
    all_to_all x1, waiting for transfers between devices, body(): lax.all_to_all(jnp.broadcast_to(partial[None], (devices, 1, ny)), ('lat',...  3.3 us
    pallas_call x1, Pallas kernels, body(): call(lambda *refs: second_kernel(0, *refs), [field, field, edge, edge, (c...  3.09 us
    pallas_call x1, Pallas kernels, body(): call(lambda *refs: first_kernel(1, *refs), [field, field, edge, edge, (cx...  3.01 us
  transfers between devices with their start and end apart: 10, of which 6 were waited for; matrix products, arithmetic and copies ran while one was open for 1% of the time, Pallas kernels for 0%

profile of v1, /device:TPU:38, one launch (start us, length us, event | category | flops | bytes accessed | tf_op | source)
XLA Modules:
  0.0 100.7 jit_solution(18039069252745289729)
XLA Ops:
  0.6 2.8 %prepare.1 = (f32[4,64,128]{2,1,0:T(8,128)}, f32[1,128]{1,0:T(1,128)}, f32[58,8,128]{2,1,0:T(8,128)}, f32[58,8,128]{2,1,0:T(8,128)}) custom-call(f32[3,4,64,128]{3,2,1,0:T(8,128)} %refs_0_.1, f32[3,4,64,128]{3,2,1,0:T(8,128)} %refs_1_.1, bf16[2,3,4,64,128]{4,3,2,1,0:T(8,128)(2,1)} %refs_2_.3, s32[4,64,128]{2,1,0:T(8,128)} %refs_3_.3, f32[64,128]{1,0:T(8,128)} %refs_7_.1, ...), custom_call_target="tpu_custom_call" | custom-call | tf_op jit(solution)/shard_map/prepare/pallas_call | solution.py:321
  4.1 0.7 broadcast_in_dim.7
  4.8 14.3 %all-to-all-start = ((f32[256,1,128]{2,1,0:T(1,128)}), f32[256,1,128]{2,1,0:T(1,128)S(1)}, u32[]{:S(2)}, u32[]{:S(2)}) async-start(f32[256,1,128]{2,1,0:T(1,128)} %broadcast_in_dim.7), calls=%async_computation | async-start | bytes 262144 | tf_op jit(solution)/shard_map/all_to_all | solution.py:337
  19.2 2.0 %collective-permute-start = (f32[58,8,128]{2,1,0:T(8,128)}, f32[58,8,128]{2,1,0:T(8,128)S(1)}, u32[]{:S(2)}, u32[]{:S(2)}) collective-permute-start(f32[58,8,128]{2,1,0:T(8,128)} %get-tuple-element.19), channel_id=1, source_target_pairs={{0,8},{8,16},{16,24},{24,32},{32,40},{40,48},{48,56},{56,64},{64,7... | collective-permute-start | bytes 712712 | tf_op jit(solution)/shard_map/ppermute | solution.py:23
  21.2 5.6 %collective-permute-start.1 = (f32[58,8,128]{2,1,0:T(8,128)S(1)}, f32[58,8,128]{2,1,0:T(8,128)S(1)}, u32[]{:S(2)}, u32[]{:S(2)}) collective-permute-start(f32[58,8,128]{2,1,0:T(8,128)S(1)} %copy-done.11), channel_id=1, source_target_pairs={{8,0},{16,8},{24,16},{32,24},{40,32},{48,40},{56,48},{64,56},{72,6... | collective-permute-start | bytes 712712 | tf_op jit(solution)/shard_map/ppermute | solution.py:23
  26.9 3.3 %all-to-all-done = f32[256,1,128]{2,1,0:T(1,128)S(1)} async-done(((f32[256,1,128]{2,1,0:T(1,128)}), f32[256,1,128]{2,1,0:T(1,128)S(1)}, u32[]{:S(2)}, u32[]{:S(2)}) %all-to-all-start) | async-done | bytes 131104 | tf_op jit(solution)/shard_map/all_to_all | solution.py:337
  31.6 3.0 %first.1 = (f32[3,4,80,128]{3,2,1,0:T(8,128)}, f32[3,4,80,128]{3,2,1,0:T(8,128)}, f32[2,80,128]{2,1,0:T(8,128)}, f32[2,80,128]{2,1,0:T(8,128)}, f32[64,128]{1,0:T(8,128)}, /*index=5*/f32[64,128]{1,0:T(8,128)}) custom-call(f32[3,4,64,128]{3,2,1,0:T(8,128)} %refs_0_.1, f32[3,4,64,128]{3,2,1,0:T(8,128)} %refs_1_.1, bf16[2,3,4,64,128]{4,3,2,1,0:T(8,128)(2,1)} %refs_2_.3, ...), custom_call_target="tpu_custom_call" | custom-call | tf_op jit(solution)/shard_map/first/pallas_call | solution.py:345
  34.6 7.3 %collective-permute-start.3 = (f32[2,80,128]{2,1,0:T(8,128)}, f32[2,80,128]{2,1,0:T(8,128)S(1)}, u32[]{:S(2)}, u32[]{:S(2)}) collective-permute-start(f32[2,80,128]{2,1,0:T(8,128)} %get-tuple-element.25), channel_id=1, source_target_pairs={{1,0},{2,1},{3,2},{4,3},{5,4},{6,5},{7,6},{9,8},{10,9},{11,10},{12... | collective-permute-start | bytes 245768 | tf_op jit(solution)/shard_map/ppermute | solution.py:23
  41.9 2.4 %collective-permute-start.2 = (f32[2,80,128]{2,1,0:T(8,128)}, f32[2,80,128]{2,1,0:T(8,128)S(1)}, u32[]{:S(2)}, u32[]{:S(2)}) collective-permute-start(f32[2,80,128]{2,1,0:T(8,128)} %get-tuple-element.24.refs_12_), channel_id=1, source_target_pairs={{0,1},{1,2},{2,3},{3,4},{4,5},{5,6},{6,7},{8,9},{9,10},{10,11},{11... | collective-permute-start | bytes 245768 | tf_op jit(solution)/shard_map/ppermute | solution.py:23
  44.3 1.7 %collective-permute-done.3.refs_11_ = f32[2,80,128]{2,1,0:T(8,128)S(1)} collective-permute-done((f32[2,80,128]{2,1,0:T(8,128)}, f32[2,80,128]{2,1,0:T(8,128)S(1)}, u32[]{:S(2)}, u32[]{:S(2)}) %collective-permute-start.3) | collective-permute-done | bytes 81952 | tf_op jit(solution)/shard_map/ppermute | solution.py:23
  46.0 8.7 %collective-permute-done.2.refs_10_ = f32[2,80,128]{2,1,0:T(8,128)S(1)} collective-permute-done((f32[2,80,128]{2,1,0:T(8,128)}, f32[2,80,128]{2,1,0:T(8,128)S(1)}, u32[]{:S(2)}, u32[]{:S(2)}) %collective-permute-start.2) | collective-permute-done | bytes 81952 | tf_op jit(solution)/shard_map/ppermute | solution.py:23
  55.3 3.1 %second.1 = (f32[3,4,80,128]{3,2,1,0:T(8,128)}, f32[3,4,80,128]{3,2,1,0:T(8,128)}, f32[2,80,128]{2,1,0:T(8,128)}, f32[2,80,128]{2,1,0:T(8,128)}, f32[64,128]{1,0:T(8,128)}) custom-call(f32[3,4,80,128]{3,2,1,0:T(8,128)} %get-tuple-element.22.refs_0_, f32[3,4,80,128]{3,2,1,0:T(8,128)} %get-tuple-element.23.refs_1_, bf16[2,3,4,64,128]{4,3,2,1,0:T(8,128)(2,1)} %refs_2_.3, ...), custom_call_target="tpu_custom_call" | custom-call | tf_op jit(solution)/shard_map/second/pallas_call | solution.py:354
  58.4 0.7 fusion
  59.1 3.9 %collective-permute-start.7 = (f32[16,128]{1,0:T(8,128)S(1)}, f32[16,128]{1,0:T(8,128)S(1)}, u32[]{:S(2)}, u32[]{:S(2)}) collective-permute-start(f32[16,128]{1,0:T(8,128)S(1)} %get-tuple-element.33), channel_id=1, source_target_pairs={{8,0},{16,8},{24,16},{32,24},{40,32},{48,40},{56,48},{64,56},{72,6... | collective-permute-start | bytes 24584 | tf_op jit(solution)/shard_map/ppermute | solution.py:23
  63.0 1.9 %collective-permute-start.6 = (f32[16,128]{1,0:T(8,128)S(1)}, f32[16,128]{1,0:T(8,128)S(1)}, u32[]{:S(2)}, u32[]{:S(2)}) collective-permute-start(f32[16,128]{1,0:T(8,128)S(1)} %get-tuple-element.34), channel_id=1, source_target_pairs={{0,8},{8,16},{16,24},{24,32},{32,40},{40,48},{48,56},{56,64},{64,7... | collective-permute-start | bytes 24584 | tf_op jit(solution)/shard_map/ppermute | solution.py:23
  65.0 5.1 %collective-permute-done.6.lo = f32[16,128]{1,0:T(8,128)S(1)} collective-permute-done((f32[16,128]{1,0:T(8,128)S(1)}, f32[16,128]{1,0:T(8,128)S(1)}, u32[]{:S(2)}, u32[]{:S(2)}) %collective-permute-start.6) | collective-permute-done | bytes 8224 | tf_op jit(solution)/shard_map/ppermute | solution.py:23
  70.7 1.8 %smooth.1 = f32[64,128]{1,0:T(8,128)} custom-call(f32[16,128]{1,0:T(8,128)} %copy-done.9, f32[64,128]{1,0:T(8,128)} %get-tuple-element.32.mid, f32[16,128]{1,0:T(8,128)} %copy-done.8), custom_call_target="tpu_custom_call" | custom-call | tf_op jit(solution)/shard_map/smooth/pallas_call | solution.py:368
  72.5 1.5 %broadcast_in_dim.16 = f32[8,64,128]{2,1,0:T(8,128)} broadcast(f32[64,128]{1,0:T(8,128)} %smooth.1), dimensions={1,2} | broadcast | bytes 294912 | tf_op jit(solution)/shard_map/broadcast_in_dim | solution.py:370
  74.0 4.9 %all-to-all-start.1 = ((f32[8,64,128]{2,1,0:T(8,128)}), f32[8,64,128]{2,1,0:T(8,128)S(1)}, u32[]{:S(2)}, u32[]{:S(2)}) async-start(f32[8,64,128]{2,1,0:T(8,128)} %broadcast_in_dim.16), calls=%async_computation.1 | async-start | bytes 524288 | tf_op jit(solution)/shard_map/all_to_all | solution.py:370
  78.9 7.6 %collective-permute-start.5 = (f32[2,80,128]{2,1,0:T(8,128)S(1)}, f32[2,80,128]{2,1,0:T(8,128)S(1)}, u32[]{:S(2)}, u32[]{:S(2)}) collective-permute-start(f32[2,80,128]{2,1,0:T(8,128)S(1)} %copy-done.12), channel_id=1, source_target_pairs={{1,0},{2,1},{3,2},{4,3},{5,4},{6,5},{7,6},{9,8},{10,9},{11,10},{12... | collective-permute-start | bytes 245768 | tf_op jit(solution)/shard_map/ppermute | solution.py:23
  86.5 2.2 %collective-permute-start.4 = (f32[2,80,128]{2,1,0:T(8,128)S(1)}, f32[2,80,128]{2,1,0:T(8,128)S(1)}, u32[]{:S(2)}, u32[]{:S(2)}) collective-permute-start(f32[2,80,128]{2,1,0:T(8,128)S(1)} %copy-done.3), channel_id=1, source_target_pairs={{0,1},{1,2},{2,3},{3,4},{4,5},{5,6},{6,7},{8,9},{9,10},{10,11},{11... | collective-permute-start | bytes 245768 | tf_op jit(solution)/shard_map/ppermute | solution.py:23
  88.7 1.6 %collective-permute-done.5.recv_hi = f32[2,80,128]{2,1,0:T(8,128)S(1)} collective-permute-done((f32[2,80,128]{2,1,0:T(8,128)S(1)}, f32[2,80,128]{2,1,0:T(8,128)S(1)}, u32[]{:S(2)}, u32[]{:S(2)}) %collective-permute-start.5) | collective-permute-done | bytes 81952 | tf_op jit(solution)/shard_map/ppermute | solution.py:23
  90.3 7.3 %collective-permute-done.4.recv_lo = f32[2,80,128]{2,1,0:T(8,128)S(1)} collective-permute-done((f32[2,80,128]{2,1,0:T(8,128)S(1)}, f32[2,80,128]{2,1,0:T(8,128)S(1)}, u32[]{:S(2)}, u32[]{:S(2)}) %collective-permute-start.4) | collective-permute-done | bytes 81952 | tf_op jit(solution)/shard_map/ppermute | solution.py:23
  98.4 2.3 %final.1 = (f32[3,4,64,128]{3,2,1,0:T(8,128)}, f32[3,4,64,128]{3,2,1,0:T(8,128)}, f32[64,128]{1,0:T(8,128)}) custom-call(f32[3,4,80,128]{3,2,1,0:T(8,128)} %get-tuple-element.28.e, f32[3,4,80,128]{3,2,1,0:T(8,128)} %get-tuple-element.29.h, f32[2,80,128]{2,1,0:T(8,128)} %copy-done.7, f32[2,80,128]{2,1,0:T(8,128)} %copy-done.5, ...), custom_call_target="tpu_custom_call" | custom-call | tf_op jit(solution)/shard_map/final/pallas_call | solution.py:371
  (32 shorter events, 4.0 us)
Async XLA Ops:
  3.4 0.7 copy-start.10
  3.4 17.8 %copy-start.11 = (f32[58,8,128]{2,1,0:T(8,128)S(1)}, f32[58,8,128]{2,1,0:T(8,128)}, u32[]{:S(2)}) copy-start(f32[58,8,128]{2,1,0:T(8,128)} %get-tuple-element.20) | copy-start | bytes 712708
  4.8 25.4 %all-to-all-start = ((f32[256,1,128]{2,1,0:T(1,128)}), f32[256,1,128]{2,1,0:T(1,128)S(1)}, u32[]{:S(2)}, u32[]{:S(2)}) async-start(f32[256,1,128]{2,1,0:T(1,128)} %broadcast_in_dim.7), calls=%async_computation | async-start | bytes 262144 | tf_op jit(solution)/shard_map/all_to_all | solution.py:337
  19.2 11.6 %collective-permute-start = (f32[58,8,128]{2,1,0:T(8,128)}, f32[58,8,128]{2,1,0:T(8,128)S(1)}, u32[]{:S(2)}, u32[]{:S(2)}) collective-permute-start(f32[58,8,128]{2,1,0:T(8,128)} %get-tuple-element.19), channel_id=1, source_target_pairs={{0,8},{8,16},{16,24},{24,32},{32,40},{40,48},{48,56},{56,64},{64,7... | collective-permute-start | bytes 712712 | tf_op jit(solution)/shard_map/ppermute | solution.py:23
  21.2 9.6 %collective-permute-start.1 = (f32[58,8,128]{2,1,0:T(8,128)S(1)}, f32[58,8,128]{2,1,0:T(8,128)S(1)}, u32[]{:S(2)}, u32[]{:S(2)}) collective-permute-start(f32[58,8,128]{2,1,0:T(8,128)S(1)} %copy-done.11), channel_id=1, source_target_pairs={{8,0},{16,8},{24,16},{32,24},{40,32},{48,40},{56,48},{64,56},{72,6... | collective-permute-start | bytes 712712 | tf_op jit(solution)/shard_map/ppermute | solution.py:23
  30.8 0.7 copy-start.1
  30.8 0.8 copy-start.2
  34.6 11.4 %collective-permute-start.3 = (f32[2,80,128]{2,1,0:T(8,128)}, f32[2,80,128]{2,1,0:T(8,128)S(1)}, u32[]{:S(2)}, u32[]{:S(2)}) collective-permute-start(f32[2,80,128]{2,1,0:T(8,128)} %get-tuple-element.25), channel_id=1, source_target_pairs={{1,0},{2,1},{3,2},{4,3},{5,4},{6,5},{7,6},{9,8},{10,9},{11,10},{12... | collective-permute-start | bytes 245768 | tf_op jit(solution)/shard_map/ppermute | solution.py:23
  41.9 12.8 %collective-permute-start.2 = (f32[2,80,128]{2,1,0:T(8,128)}, f32[2,80,128]{2,1,0:T(8,128)S(1)}, u32[]{:S(2)}, u32[]{:S(2)}) collective-permute-start(f32[2,80,128]{2,1,0:T(8,128)} %get-tuple-element.24.refs_12_), channel_id=1, source_target_pairs={{0,1},{1,2},{2,3},{3,4},{4,5},{5,6},{6,7},{8,9},{9,10},{10,11},{11... | collective-permute-start | bytes 245768 | tf_op jit(solution)/shard_map/ppermute | solution.py:23
  46.0 8.7 %copy-start.4 = (f32[2,80,128]{2,1,0:T(8,128)}, f32[2,80,128]{2,1,0:T(8,128)S(1)}, u32[]{:S(2)}) copy-start(f32[2,80,128]{2,1,0:T(8,128)S(1)} %collective-permute-done.3.refs_11_) | copy-start | bytes 245764
  54.7 0.6 copy-start.6
  59.1 5.8 %collective-permute-start.7 = (f32[16,128]{1,0:T(8,128)S(1)}, f32[16,128]{1,0:T(8,128)S(1)}, u32[]{:S(2)}, u32[]{:S(2)}) collective-permute-start(f32[16,128]{1,0:T(8,128)S(1)} %get-tuple-element.33), channel_id=1, source_target_pairs={{8,0},{16,8},{24,16},{32,24},{40,32},{48,40},{56,48},{64,56},{72,6... | collective-permute-start | bytes 24584 | tf_op jit(solution)/shard_map/ppermute | solution.py:23
  63.0 7.1 %collective-permute-start.6 = (f32[16,128]{1,0:T(8,128)S(1)}, f32[16,128]{1,0:T(8,128)S(1)}, u32[]{:S(2)}, u32[]{:S(2)}) collective-permute-start(f32[16,128]{1,0:T(8,128)S(1)} %get-tuple-element.34), channel_id=1, source_target_pairs={{0,8},{8,16},{16,24},{24,32},{32,40},{40,48},{48,56},{56,64},{64,7... | collective-permute-start | bytes 24584 | tf_op jit(solution)/shard_map/ppermute | solution.py:23
  65.0 5.1 %copy-start.8 = (f32[16,128]{1,0:T(8,128)}, f32[16,128]{1,0:T(8,128)S(1)}, u32[]{:S(2)}) copy-start(f32[16,128]{1,0:T(8,128)S(1)} %collective-permute-done.7.hi) | copy-start | bytes 24580
  70.1 0.6 copy-start.9
  74.0 5.0 %copy-start.12 = (f32[2,80,128]{2,1,0:T(8,128)S(1)}, f32[2,80,128]{2,1,0:T(8,128)}, u32[]{:S(2)}) copy-start(f32[2,80,128]{2,1,0:T(8,128)} %get-tuple-element.31) | copy-start | bytes 245764
  74.0 12.5 %copy-start.3 = (f32[2,80,128]{2,1,0:T(8,128)S(1)}, f32[2,80,128]{2,1,0:T(8,128)}, u32[]{:S(2)}) copy-start(f32[2,80,128]{2,1,0:T(8,128)} %get-tuple-element.30.up) | copy-start | bytes 245764
  74.0 23.7 %all-to-all-start.1 = ((f32[8,64,128]{2,1,0:T(8,128)}), f32[8,64,128]{2,1,0:T(8,128)S(1)}, u32[]{:S(2)}, u32[]{:S(2)}) async-start(f32[8,64,128]{2,1,0:T(8,128)} %broadcast_in_dim.16), calls=%async_computation.1 | async-start | bytes 524288 | tf_op jit(solution)/shard_map/all_to_all | solution.py:370
  78.9 11.4 %collective-permute-start.5 = (f32[2,80,128]{2,1,0:T(8,128)S(1)}, f32[2,80,128]{2,1,0:T(8,128)S(1)}, u32[]{:S(2)}, u32[]{:S(2)}) collective-permute-start(f32[2,80,128]{2,1,0:T(8,128)S(1)} %copy-done.12), channel_id=1, source_target_pairs={{1,0},{2,1},{3,2},{4,3},{5,4},{6,5},{7,6},{9,8},{10,9},{11,10},{12... | collective-permute-start | bytes 245768 | tf_op jit(solution)/shard_map/ppermute | solution.py:23
  86.5 11.1 %collective-permute-start.4 = (f32[2,80,128]{2,1,0:T(8,128)S(1)}, f32[2,80,128]{2,1,0:T(8,128)S(1)}, u32[]{:S(2)}, u32[]{:S(2)}) collective-permute-start(f32[2,80,128]{2,1,0:T(8,128)S(1)} %copy-done.3), channel_id=1, source_target_pairs={{0,1},{1,2},{2,3},{3,4},{4,5},{5,6},{6,7},{8,9},{9,10},{10,11},{11... | collective-permute-start | bytes 245768 | tf_op jit(solution)/shard_map/ppermute | solution.py:23
  90.3 7.3 %copy-start.5 = (f32[2,80,128]{2,1,0:T(8,128)}, f32[2,80,128]{2,1,0:T(8,128)S(1)}, u32[]{:S(2)}) copy-start(f32[2,80,128]{2,1,0:T(8,128)S(1)} %collective-permute-done.5.recv_hi) | copy-start | bytes 245764
  97.6 0.6 copy-start.7
  97.7 0.7 copy-start

commit v2 on v1

v2 whole, which is shorter than its diff:
```python
import jax
import jax.numpy as jnp
from jax import lax
from jax.experimental import pallas as pl
from jax.experimental.pallas import tpu as pltpu
from jax.sharding import PartitionSpec as P

RADIUS = 16
PAD = 8

sharpness = 8.0
threshold = 0.5
time_step = 0.5
epsilon = 1e-05

F32 = jnp.float32
VMEM = pl.BlockSpec(memory_space=pltpu.VMEM)
SMEM = pl.BlockSpec(memory_space=pltpu.SMEM)
PLANE = 72
SCOPED = 12 << 20


def inner_swap(value, axis):
    return lax.ppermute(value, axis, [(i, i ^ 1) for i in range(lax.axis_size(axis))])


def outer_swap(value, axis):
    count = lax.axis_size(axis)
    pairs = [(i, i + 1 if i % 2 else i - 1) for i in range(1, count - 1)]
    return lax.ppermute(value, axis, pairs)


def is_even(axis):
    return lax.axis_index(axis) % 2 == 0


def lower_y(v):
    lane = lax.broadcasted_iota(jnp.int32, v.shape, 1)
    return jnp.where(lane == 0, 0.0, pltpu.roll(v, 1, 1))


def upper_y(v):
    lane = lax.broadcasted_iota(jnp.int32, v.shape, 1)
    last = v.shape[1] - 1
    return jnp.where(lane == last, 0.0, pltpu.roll(v, last, 1))


def lower_x(v):
    return pltpu.roll(v, 1, 0)


def upper_x(v):
    return pltpu.roll(v, v.shape[0] - 1, 0)


def smooth(padded, rows):
    cols = padded.shape[1]
    tall = padded.shape[0]

    def cone(offset):
        return jnp.maximum(RADIUS + 1 - jnp.abs(offset), 0).astype(F32)

    a = lax.broadcasted_iota(jnp.int32, (cols, cols), 0)
    b = lax.broadcasted_iota(jnp.int32, (cols, cols), 1)
    across = jnp.dot(
        padded, cone(a - b), precision=lax.Precision.HIGHEST, preferred_element_type=F32
    )
    r = lax.broadcasted_iota(jnp.int32, (rows, tall), 0)
    s = lax.broadcasted_iota(jnp.int32, (rows, tall), 1)
    down = jnp.dot(
        cone(s - RADIUS - r), across, precision=lax.Precision.HIGHEST, preferred_element_type=F32
    )
    return down * (1.0 / (RADIUS + 1) ** 4)


def prepare_kernel(e, h, sv, labels, density, cells, weight, w_out, spread, inner, outer):
    cz, cx, ny = labels.shape
    count = cells.shape[1]
    even = is_even("lat")

    def send(slot, rows):
        last = rows[rows.shape[0] - PAD :]
        first = rows[:PAD]
        inner[slot] = jnp.where(even, last, first)
        outer[slot] = jnp.where(even, first, last)

    cell = cells[...]
    row = cell // ny
    col = cell % ny
    rows_hot = jnp.where(
        lax.broadcasted_iota(jnp.int32, (cz * cx, count), 0) == row, weight[...], 0.0
    )
    cols_hot = (lax.broadcasted_iota(jnp.int32, (ny, count), 0) == col).astype(F32)
    w = lax.dot_general(
        rows_hot,
        cols_hot,
        (((1,), (1,)), ((), ())),
        precision=lax.Precision.HIGHEST,
        preferred_element_type=F32,
    ).reshape(cz, cx, ny)
    w_out[...] = w
    steps = sv.shape[0]
    lane = lax.broadcasted_iota(jnp.int32, (1, ny), 1)
    packed = jnp.zeros((1, ny), F32)
    for k in range(steps):
        total = jnp.zeros((cx, ny), F32)
        for z in range(cz):
            square = jnp.zeros((cx, ny), F32)
            for c in range(3):
                f = sv[k, c, z].astype(F32)
                square = square + f * f
                send((1 + 2 * (steps - 1 - k)) * 3 * cz + c * cz + z, f)
            total = total + w[z] * square
        packed = jnp.where(lane == k, jnp.sum(total), packed)
    spread[...] = jnp.broadcast_to(packed[None], spread.shape)
    for z in range(cz):
        for c in range(3):
            send(c * cz + z, e.at[c, z])
            send((6 + c) * cz + z, h.at[c, z])
        send(12 * cz + z, labels[z].astype(F32))
        send(13 * cz + z, w[z])
    tiles = RADIUS // PAD
    for t in range(tiles):
        last = density[cx - RADIUS + t * PAD : cx - RADIUS + (t + 1) * PAD]
        first = density[t * PAD : (t + 1) * PAD]
        inner[14 * cz + t] = jnp.where(even, last, first)
        outer[14 * cz + t] = jnp.where(even, first, last)


class Sides:
    def __init__(self, inner, outer):
        self.inner, self.outer, self.even = inner, outer, is_even("lat")

    def both(self, slot):
        a, b = self.inner[slot], self.outer[slot]
        return jnp.where(self.even, b, a), jnp.where(self.even, a, b)

    def wrap(self, slot, mid):
        lo, hi = self.both(slot)
        return jnp.concatenate([lo, mid, hi], 0)


def derivative_kernel(density, inner, outer, out):
    cx, ny = density.shape
    tiles = RADIUS // PAD
    sides = Sides(inner, outer)
    base = inner.shape[0] - tiles
    pairs = [sides.both(base + t) for t in range(tiles)]
    padded = jnp.concatenate([p[0] for p in pairs] + [density[...]] + [p[1] for p in pairs], 0)
    slope = jnp.tanh(sharpness * (smooth(padded, cx) - threshold))
    scale = jnp.tanh(jnp.full((1, ny), sharpness * threshold, F32)) + jnp.tanh(
        jnp.full((1, ny), sharpness * (1.0 - threshold), F32)
    )
    out[...] = sharpness * (1.0 - slope * slope) / scale


def source_and_lower(
    k, get_e, get_h, put_e, put_h, sv, labels, w, sides, eps_t, chi_t, inv_power, s, mask_s, mask_h
):
    cz, cx, ny = labels.shape
    steps = sv.shape[0]
    base = (1 + 2 * (steps - 1 - k)) * 3 * cz
    plane = jnp.zeros((cx, ny), F32)
    for z in range(cz):
        lab = sides.wrap(12 * cz + z, labels[z].astype(F32))
        eps = jnp.full(lab.shape, eps_t[0], F32)
        chi = jnp.full(lab.shape, 3.0 * chi_t[0], F32)
        for r in range(1, eps_t.shape[0]):
            eps = jnp.where(lab == float(r), eps_t[r], eps)
            chi = jnp.where(lab == float(r), 3.0 * chi_t[r], chi)
        wz = sides.wrap(13 * cz + z, w[z]) * inv_power
        along = jnp.zeros((cx, ny), F32)
        for c in range(3):
            f = sides.wrap(base + c * cz + z, sv[k, c, z].astype(F32))
            ec = get_e(c, z) + wz * f
            put_e(c, z, ec)
            sc = ec / (eps + chi * f * f)
            if mask_s is not None:
                sc = sc * mask_s
            s[c, z] = sc
            along = along + (sc * f)[PAD : PAD + cx]
        plane = plane + jnp.where(lab[PAD : PAD + cx] == 0.0, along, 0.0)
    for z in range(cz):
        sx, sy, sz = s[0, z], s[1, z], s[2, z]
        curl_x = sz - lower_y(sz) - sy
        curl_y = sx - sz + lower_x(sz)
        curl_z = sy - lower_x(sy) - sx + lower_y(sx)
        if z > 0:
            curl_x = curl_x + s[1, z - 1]
            curl_y = curl_y - s[0, z - 1]
        for c, curl in enumerate((curl_x, curl_y, curl_z)):
            put_h(c, z, (get_h(c, z) - time_step * curl) * mask_h)
    return plane


def row_masks(tall, cx):
    row = lax.broadcasted_iota(jnp.int32, (tall, 128), 0)
    lat = lax.axis_index("lat")
    first = jnp.where(lat == 0, PAD, 0)
    last = jnp.where(lat == lax.axis_size("lat") - 1, PAD + cx, tall)
    mask_s = jnp.where(row >= first, 1.0, 0.0)
    mask_h = jnp.where(row < last, 1.0, 0.0)
    return mask_s, mask_h


def pack_edges(s, h, inner, outer):
    cz, tall = s.shape[1], s.shape[2]
    own = tall - 2 * PAD
    even = is_even("ha")
    row = lax.broadcasted_iota(jnp.int32, (PAD, s.shape[3]), 0)
    for c in range(2):
        up, down = s[c, cz - 1], h[c, 0]
        for start, a, b in (
            (0, up[PAD : PAD + own], down[PAD : PAD + own]),
            (
                own,
                jnp.where(row == PAD - 1, up[:PAD], up[PAD + own :]),
                jnp.where(row == PAD - 1, down[:PAD], down[PAD + own :]),
            ),
        ):
            at = pl.ds(c * PLANE + start, a.shape[0])
            inner[at] = jnp.where(even, a, b)
            outer[at] = jnp.where(even, b, a)


def unpack_edges(inner, outer):
    even = is_even("ha")
    below, above = [], []
    for c in range(2):
        a = inner[pl.ds(c * PLANE, PLANE)]
        b = outer[pl.ds(c * PLANE, PLANE)]
        own = PLANE - PAD
        for out, v in ((below, jnp.where(even, b, a)), (above, jnp.where(even, a, b))):
            out.append(jnp.concatenate([v[own:], v[:own], v[own:]], 0))
    return below, above


def completed(h, s_top, inner, outer, mask_h):
    cz = h.shape[1]
    below, above = unpack_edges(inner, outer)
    top = jnp.where(lax.axis_index("ha") == lax.axis_size("ha") - 1, 0.0, 1.0)
    low = (
        h[0, 0] - time_step * (below[1] * mask_h),
        h[1, 0] + time_step * (below[0] * mask_h),
    )
    high = (
        (above[0] - time_step * (s_top[1] * mask_h)) * top,
        (above[1] + time_step * (s_top[0] * mask_h)) * top,
    )

    def layer(c, z):
        if z == 0 and c < 2:
            return low[c]
        return high[c] if z == cz else h[c, z]

    return layer


def upper_curl(layer, z):
    hx, hy, hz = (layer(c, z) for c in range(3))
    above_x, above_y = layer(0, z + 1), layer(1, z + 1)
    return (
        upper_y(hz) - hz - (above_y - hy),
        above_x - hx - (upper_x(hz) - hz),
        upper_x(hy) - hy - (upper_y(hx) - hx),
    )


def first_kernel(
    k, count_all, e, h, sv, labels, w, inner, outer, spread, eps_t, chi_t,
    e_out, h_out, top_out, plane_out, inv_out, send_inner, send_outer, s,
):
    cz, cx, ny = labels.shape
    tall = e_out.shape[2]
    _, mask_h = row_masks(tall, cx)
    sides = Sides(inner, outer)
    inv = 1.0 / (jnp.sum(spread[...], 0) / count_all + epsilon)
    inv_out[...] = inv

    def get_e(c, z):
        return sides.wrap(c * cz + z, e[c, z])

    def get_h(c, z):
        return sides.wrap((6 + c) * cz + z, h[c, z])

    def put_e(c, z, v):
        e_out[c, z] = v

    def put_h(c, z, v):
        h_out[c, z] = v

    plane_out[...] = source_and_lower(
        k, get_e, get_h, put_e, put_h, sv, labels, w, sides, eps_t, chi_t,
        inv[:, k : k + 1], s, None, mask_h,
    )
    for c in range(2):
        top_out[c] = s[c, cz - 1]
    pack_edges(s, h_out, send_inner, send_outer)


def second_kernel(
    k, e, h, s_top, plane, inv, deriv, sv, labels, w, inner, outer, edge_inner, edge_outer, eps_t, chi_t,
    e_out, h_out, top_out, send_inner, send_outer, s, e1,
):
    cz, cx, ny = labels.shape
    tall = e.shape[2]
    mask_s, mask_h = row_masks(tall, cx)
    layer = completed(h, s_top, edge_inner, edge_outer, mask_h)
    for z in range(cz):
        curls = upper_curl(layer, z)
        for c in range(3):
            e1[c, z] = e[c, z] + time_step * curls[c]

    def get_e(c, z):
        return e1[c, z]

    def put_e(c, z, v):
        e_out[c, z] = v

    def put_h(c, z, v):
        h_out[c, z] = v

    total = plane[...] + source_and_lower(
        k, get_e, layer, put_e, put_h, sv, labels, w, Sides(inner, outer), eps_t, chi_t,
        inv[:, k : k + 1], s, mask_s, mask_h,
    )
    for c in range(2):
        top_out[c] = s[c, cz - 1]
    pack_edges(s, h_out, send_inner, send_outer)
    send_inner[pl.ds(2 * PLANE, cx)] = total * deriv[...]


def pair_kernel(mine, other, out):
    rows = out.shape[1]
    at = pl.ds(mine.shape[0] - rows, rows)
    both = mine[at] + other[at]
    for i in range(out.shape[0]):
        out[i] = both


def total_kernel(parts, out, inner, outer):
    total = parts[0]
    for i in range(1, parts.shape[0]):
        total = total + parts[i]
    out[...] = total
    even = is_even("lat")
    first, last = total[:RADIUS], total[total.shape[0] - RADIUS :]
    inner[...] = jnp.where(even, last, first)
    outer[...] = jnp.where(even, first, last)


def fields_kernel(e, h, s_top, inner, outer, e_out, h_out):
    cz = h.shape[1]
    tall = e.shape[2]
    cx = e_out.shape[2]
    own = slice(PAD, PAD + cx)
    _, mask_h = row_masks(tall, cx)
    layer = completed(h, s_top, inner, outer, mask_h)
    for z in range(cz):
        curls = upper_curl(layer, z)
        for c in range(3):
            e_out[c, z] = (e[c, z] + time_step * curls[c])[own]
            h_out[c, z] = layer(c, z)[own]


def smooth_kernel(mid, inner, outer, out):
    even = is_even("lat")
    a, b = inner[...], outer[...]
    padded = jnp.concatenate([jnp.where(even, b, a), mid[...], jnp.where(even, a, b)], 0)
    out[...] = smooth(padded, mid.shape[0])


def call(kernel, args, outs, name, tables=(), scratch=(), keep=True, held=True):
    if held:
        args = [pltpu.with_memory_space_constraint(a, pltpu.VMEM) for a in args]
    out = [pltpu.VMEM(o, F32) if keep else jax.ShapeDtypeStruct(o, F32) for o in outs]
    return pl.pallas_call(
        kernel,
        out_shape=out,
        in_specs=[VMEM] * len(args) + [SMEM] * len(tables),
        out_specs=[VMEM] * len(outs),
        scratch_shapes=[pltpu.VMEM(x, F32) for x in scratch],
        compiler_params=pltpu.CompilerParams(vmem_limit_bytes=SCOPED),
        name=name,
    )(*args, *tables)


def body(
    adjoint_e, adjoint_h, saved_e, labels, eps_table, chi_table, density, mon_cells, mon_weight
):
    cz, cx, ny = labels.shape
    tall = cx + 2 * PAD
    devices = lax.axis_size("lat") * lax.axis_size("ha")
    count_all = mon_cells.shape[0] * devices
    halo = (14 * cz + RADIUS // PAD, PAD, ny)
    tables = (eps_table, chi_table)

    w, partial, inner, outer = call(
        prepare_kernel,
        [
            adjoint_e,
            adjoint_h,
            saved_e,
            labels,
            density,
            mon_cells.reshape(1, -1),
            mon_weight.reshape(1, -1),
        ],
        [(cz, cx, ny), (devices, 1, ny), halo, halo],
        "prepare",
        held=False,
    )
    inner = inner_swap(inner, "lat")
    outer = outer_swap(outer, "lat")
    spread = lax.all_to_all(partial, ("lat", "ha"), 0, 0)

    field = (3, cz, tall, ny)
    edge = (2, tall, ny)
    e1, h1, top1, plane1, inv, edge_inner, edge_outer = call(
        lambda *refs: first_kernel(1, count_all, *refs),
        [adjoint_e, adjoint_h, saved_e, labels, w, inner, outer, spread],
        [field, field, edge, (cx, ny), (1, ny), (2 * PLANE, ny), (2 * PLANE, ny)],
        "first",
        tables,
        [field],
    )
    edge_inner = inner_swap(edge_inner, "ha")
    edge_outer = outer_swap(edge_outer, "ha")
    (deriv,) = call(derivative_kernel, [density, inner, outer], [(cx, ny)], "derivative")
    e0, h0, top0, mine, edge_outer = call(
        lambda *refs: second_kernel(0, *refs),
        [e1, h1, top1, plane1, inv, deriv, saved_e, labels, w, inner, outer, edge_inner, edge_outer],
        [field, field, edge, (2 * PLANE + cx, ny), (2 * PLANE, ny)],
        "second",
        tables,
        [field, field],
    )
    edge_inner = inner_swap(mine, "ha")
    edge_outer = outer_swap(edge_outer, "ha")
    members = lax.axis_size("ha") // 2
    (both,) = call(pair_kernel, [mine, edge_inner], [(members, cx, ny)], "pair")
    groups = [[2 * i + j for i in range(members)] for j in range(2)]
    parts = lax.all_to_all(both, "ha", 0, 0, axis_index_groups=groups)
    total, side_inner, side_outer = call(
        total_kernel, [parts], [(cx, ny), (RADIUS, ny), (RADIUS, ny)], "total"
    )
    side_inner = inner_swap(side_inner, "lat")
    side_outer = outer_swap(side_outer, "lat")
    final_e, final_h = call(
        fields_kernel,
        [e0, h0, top0, edge_inner, edge_outer],
        [adjoint_e.shape, adjoint_h.shape],
        "fields",
        keep=False,
    )
    (grad,) = call(smooth_kernel, [total, side_inner, side_outer], [(cx, ny)], "smooth", keep=False)
    return (final_e, final_h, grad)


def solution(mesh):
    return jax.shard_map(
        body,
        mesh=mesh,
        in_specs=(
            P(None, "ha", "lat", None),
            P(None, "ha", "lat", None),
            P(None, None, "ha", "lat", None),
            P("ha", "lat", None),
            P(),
            P(),
            P("lat", None),
            P(("lat", "ha")),
            P(("lat", "ha")),
        ),
        out_specs=(P(None, "ha", "lat", None), P(None, "ha", "lat", None), P("lat", None)),
        check_vma=False,
    )
```

time: 101 us -> 81.7 us (0.81)
  the two profiles are of different devices: /device:TPU:38 before, /device:TPU:25 now
where the time goes in v2:
time: 81.7 us; the launch traced here: 81.1 us
  starting transfers between devices  49.6 us (61%)
  waiting for transfers between devices  17.7 us (22%)
  Pallas kernels  7.01 us (9%)
  local copies, waits for them, and re-layouts  6.03 us (7%)
    ppermute x4, starting transfers between devices, inner_swap(): lax.ppermute(value, axis, [(i, i ^ 1) for i in range(lax.axis_size(axis))])  16.8 us
    all_to_all x1, starting transfers between devices, body(): spread = lax.all_to_all(partial, ('lat', 'ha'), 0, 0)  14.7 us
    all_to_all x1, starting transfers between devices, body(): parts = lax.all_to_all(both, 'ha', 0, 0, axis_index_groups=groups)  10.9 us
    ppermute x4, waiting for transfers between devices, outer_swap(): return lax.ppermute(value, axis, pairs)  10.2 us
    ppermute x4, starting transfers between devices, outer_swap(): return lax.ppermute(value, axis, pairs)  7.25 us
    pallas_call x8, Pallas kernels, call(): pl.pallas_call(kernel, out_shape=out, in_specs=[VMEM] * len(args) + [SMEM...  7.01 us
    unnamed x28, local copies, waits for them, and re-layouts  6.03 us
    all_to_all x1, waiting for transfers between devices, body(): parts = lax.all_to_all(both, 'ha', 0, 0, axis_index_groups=groups)  4.17 us
  transfers between devices with their start and end apart: 10, of which 6 were waited for; matrix products, arithmetic and copies ran while one was open for 0% of the time, Pallas kernels for 2%

profile of v2, /device:TPU:25, one launch (start us, length us, event | category | flops | bytes accessed | tf_op | source)
XLA Modules:
  0.0 81.1 jit_solution(5269712380456457054)
XLA Ops:
  0.6 0.7 copy-done.10
  1.3 1.0 %copy-done = bf16[2,3,4,64,128]{4,3,2,1,0:T(8,128)(2,1)S(1)} copy-done((bf16[2,3,4,64,128]{4,3,2,1,0:T(8,128)(2,1)S(1)}, bf16[2,3,4,64,128]{4,3,2,1,0:T(8,128)(2,1)}, u32[]{:S(2)}) %copy-start) | copy-done | bytes 393240
  2.3 1.0 %copy-done.2 = f32[3,4,64,128]{3,2,1,0:T(8,128)S(1)} copy-done((f32[3,4,64,128]{3,2,1,0:T(8,128)S(1)}, f32[3,4,64,128]{3,2,1,0:T(8,128)}, u32[]{:S(2)}) %copy-start.2) | copy-done | bytes 393240
  3.3 1.0 %copy-done.4 = f32[3,4,64,128]{3,2,1,0:T(8,128)S(1)} copy-done((f32[3,4,64,128]{3,2,1,0:T(8,128)S(1)}, f32[3,4,64,128]{3,2,1,0:T(8,128)}, u32[]{:S(2)}) %copy-start.4) | copy-done | bytes 393240
  4.3 0.9 %copy-done.6 = s32[4,64,128]{2,1,0:T(8,128)S(1)} copy-done((s32[4,64,128]{2,1,0:T(8,128)S(1)}, s32[4,64,128]{2,1,0:T(8,128)}, u32[]{:S(2)}) %copy-start.6) | copy-done | bytes 131096
  5.2 0.8 copy-done.8
  6.0 0.7 copy-done.11
  6.7 1.5 %prepare.1 = (f32[4,64,128]{2,1,0:T(8,128)S(1)}, f32[256,1,128]{2,1,0:T(1,128)}, f32[58,8,128]{2,1,0:T(8,128)S(1)}, f32[58,8,128]{2,1,0:T(8,128)S(1)}) custom-call(f32[3,4,64,128]{3,2,1,0:T(8,128)S(1)} %copy-done.2, f32[3,4,64,128]{3,2,1,0:T(8,128)S(1)} %copy-done.4, bf16[2,3,4,64,128]{4,3,2,1,0:T(8,128)(2,1)S(1)} %copy-done, s32[4,64,128]{2,1,0:T(8,128)S(1)} %copy-done.6, ...), custom_call_target="tpu_custom_call" | custom-call | tf_op jit(solution)/shard_map/prepare/pallas_call | solution.py:377
  8.2 14.7 %all-to-all-start = ((f32[256,1,128]{2,1,0:T(1,128)}), f32[256,1,128]{2,1,0:T(1,128)S(1)}, u32[]{:S(2)}, u32[]{:S(2)}) async-start(f32[256,1,128]{2,1,0:T(1,128)} %get-tuple-element.27), calls=%async_computation | async-start | bytes 262144 | tf_op jit(solution)/shard_map/all_to_all | solution.py:415
  23.4 3.3 %collective-permute-start.1 = (f32[58,8,128]{2,1,0:T(8,128)S(1)}, f32[58,8,128]{2,1,0:T(8,128)S(1)}, u32[]{:S(2)}, u32[]{:S(2)}) collective-permute-start(f32[58,8,128]{2,1,0:T(8,128)S(1)} %get-tuple-element.26), channel_id=1, source_target_pairs={{8,16},{16,8},{24,32},{32,24},{40,48},{48,40},{56,64},{64,56},{72,... | collective-permute-start | bytes 712712 | tf_op jit(solution)/shard_map/ppermute | solution.py:30
  26.7 6.8 %collective-permute-done.1.refs_6_.outer.refs_10_ = f32[58,8,128]{2,1,0:T(8,128)S(1)} collective-permute-done((f32[58,8,128]{2,1,0:T(8,128)S(1)}, f32[58,8,128]{2,1,0:T(8,128)S(1)}, u32[]{:S(2)}, u32[]{:S(2)}) %collective-permute-start.1) | collective-permute-done | bytes 237600 | tf_op jit(solution)/shard_map/ppermute | solution.py:30
  33.9 1.3 %first.1 = (f32[3,4,80,128]{3,2,1,0:T(8,128)S(1)}, f32[3,4,80,128]{3,2,1,0:T(8,128)S(1)}, f32[2,80,128]{2,1,0:T(8,128)S(1)}, f32[64,128]{1,0:T(8,128)S(1)}, f32[...) custom-call(f32[3,4,64,128]{3,2,1,0:T(8,128)S(1)} %copy-done.3, f32[3,4,64,128]{3,2,1,0:T(8,128)S(1)} %copy-done.5, ...), custom_call_target="tpu_custom_call" | custom-call | tf_op jit(solution)/shard_map/first/pallas_call | solution.py:377
  35.2 5.4 %collective-permute-start.2 = (f32[144,128]{1,0:T(8,128)S(1)}, f32[144,128]{1,0:T(8,128)S(1)}, u32[]{:S(2)}, u32[]{:S(2)}) collective-permute-start(f32[144,128]{1,0:T(8,128)S(1)} %get-tuple-element.33), channel_id=1, source_target_pairs={{0,1},{1,0},{2,3},{3,2},{4,5},{5,4},{6,7},{7,6},{8,9},{9,8},{10,11... | collective-permute-start | bytes 221192 | tf_op jit(solution)/shard_map/ppermute | solution.py:24
  41.7 0.8 collective-permute-done.2.refs_11_
  42.5 1.1 %second.1 = (f32[3,4,80,128]{3,2,1,0:T(8,128)S(1)}, f32[3,4,80,128]{3,2,1,0:T(8,128)S(1)}, f32[2,80,128]{2,1,0:T(8,128)S(1)}, f32[208,128]{1,0:T(8,128)S(1)}, f32[144,128]{1,0:T(8,128)S(1)}) custom-call(f32[3,4,80,128]{3,2,1,0:T(8,128)S(1)} %get-tuple-element.28.refs_0_, f32[3,4,80,128]{3,2,1,0:T(8,128)S(1)} %get-tuple-element.29.refs_1_, ...), custom_call_target="tpu_custom_call" | custom-call | tf_op jit(solution)/shard_map/second/pallas_call | solution.py:377
  43.6 8.5 %collective-permute-start.4 = (f32[208,128]{1,0:T(8,128)S(1)}, f32[208,128]{1,0:T(8,128)S(1)}, u32[]{:S(2)}, u32[]{:S(2)}) collective-permute-start(f32[208,128]{1,0:T(8,128)S(1)} %get-tuple-element.38.mine), channel_id=1, source_target_pairs={{0,1},{1,0},{2,3},{3,2},{4,5},{5,4},{6,7},{7,6},{8,9},{9,8},{10,11... | collective-permute-start | bytes 319496 | tf_op jit(solution)/shard_map/ppermute | solution.py:24
  52.1 2.1 %collective-permute-done.4.inner.other = f32[208,128]{1,0:T(8,128)S(1)} collective-permute-done((f32[208,128]{1,0:T(8,128)S(1)}, f32[208,128]{1,0:T(8,128)S(1)}, u32[]{:S(2)}, u32[]{:S(2)}) %collective-permute-start.4) | collective-permute-done | bytes 106528 | tf_op jit(solution)/shard_map/ppermute | solution.py:24
  54.9 10.9 %all-to-all-start.1 = ((f32[4,64,128]{2,1,0:T(8,128)}), f32[4,64,128]{2,1,0:T(8,128)S(1)}, u32[]{:S(2)}, u32[]{:S(2)}) async-start(f32[4,64,128]{2,1,0:T(8,128)} %pair.1), calls=%async_computation.1 | async-start | bytes 262144 | tf_op jit(solution)/shard_map/all_to_all | solution.py:443
  66.4 4.2 %all-to-all-done.1.parts = f32[4,64,128]{2,1,0:T(8,128)S(1)} async-done(((f32[4,64,128]{2,1,0:T(8,128)}), f32[4,64,128]{2,1,0:T(8,128)S(1)}, u32[]{:S(2)}, u32[]{:S(2)}) %all-to-all-start.1) | async-done | bytes 131104 | tf_op jit(solution)/shard_map/all_to_all | solution.py:443
  70.6 2.4 %collective-permute-start.6 = (f32[16,128]{1,0:T(8,128)S(1)}, f32[16,128]{1,0:T(8,128)S(1)}, u32[]{:S(2)}, u32[]{:S(2)}) collective-permute-start(f32[16,128]{1,0:T(8,128)S(1)} %get-tuple-element.43), channel_id=1, source_target_pairs={{0,8},{8,0},{16,24},{24,16},{32,40},{40,32},{48,56},{56,48},{64,72... | collective-permute-start | bytes 24584 | tf_op jit(solution)/shard_map/ppermute | solution.py:24
  73.0 2.7 %collective-permute-start.7 = (f32[16,128]{1,0:T(8,128)S(1)}, f32[16,128]{1,0:T(8,128)S(1)}, u32[]{:S(2)}, u32[]{:S(2)}) collective-permute-start(f32[16,128]{1,0:T(8,128)S(1)} %get-tuple-element.44), channel_id=1, source_target_pairs={{8,16},{16,8},{24,32},{32,24},{40,48},{48,40},{56,64},{64,56},{72,... | collective-permute-start | bytes 24584 | tf_op jit(solution)/shard_map/ppermute | solution.py:30
  75.7 1.0 %fields.1 = (f32[3,4,64,128]{3,2,1,0:T(8,128)}, f32[3,4,64,128]{3,2,1,0:T(8,128)}) custom-call(f32[3,4,80,128]{3,2,1,0:T(8,128)S(1)} %get-tuple-element.35.e, f32[3,4,80,128]{3,2,1,0:T(8,128)S(1)} %get-tuple-element.36.h, f32[2,80,128]{2,1,0:T(8,128)S(1)} %get-tuple-element.37.s_top, f32[208,128]{1,0:T(8,128)S(1)} %collective-permute-done.4.inner.other, ...), custom_call_target="tpu_custom_call" | custom-call | tf_op jit(solution)/shard_map/fields/pallas_call | solution.py:377
  76.7 3.4 %collective-permute-done.7.outer = f32[16,128]{1,0:T(8,128)S(1)} collective-permute-done((f32[16,128]{1,0:T(8,128)S(1)}, f32[16,128]{1,0:T(8,128)S(1)}, u32[]{:S(2)}, u32[]{:S(2)}) %collective-permute-start.7) | collective-permute-done | bytes 8224 | tf_op jit(solution)/shard_map/ppermute | solution.py:30
  80.1 1.0 %smooth.1 = f32[64,128]{1,0:T(8,128)} custom-call(f32[64,128]{1,0:T(8,128)S(1)} %get-tuple-element.42.mid, f32[16,128]{1,0:T(8,128)S(1)} %collective-permute-done.6.inner, f32[16,128]{1,0:T(8,128)S(1)} %collective-permute-done.7.outer), custom_call_target="tpu_custom_call" | custom-call | tf_op jit(solution)/shard_map/smooth/pallas_call | solution.py:377
  (32 shorter events, 3.3 us)
Async XLA Ops:
  0.6 0.7 copy-start.10
  1.3 1.0 %copy-start = (bf16[2,3,4,64,128]{4,3,2,1,0:T(8,128)(2,1)S(1)}, bf16[2,3,4,64,128]{4,3,2,1,0:T(8,128)(2,1)}, u32[]{:S(2)}) copy-start(bf16[2,3,4,64,128]{4,3,2,1,0:T(8,128)(2,1)} %refs_6_.1) | copy-start | bytes 1179652
  2.3 1.0 %copy-start.2 = (f32[3,4,64,128]{3,2,1,0:T(8,128)S(1)}, f32[3,4,64,128]{3,2,1,0:T(8,128)}, u32[]{:S(2)}) copy-start(f32[3,4,64,128]{3,2,1,0:T(8,128)} %refs_0_.1) | copy-start | bytes 1179652
  3.3 1.0 %copy-start.4 = (f32[3,4,64,128]{3,2,1,0:T(8,128)S(1)}, f32[3,4,64,128]{3,2,1,0:T(8,128)}, u32[]{:S(2)}) copy-start(f32[3,4,64,128]{3,2,1,0:T(8,128)} %refs_1_.1) | copy-start | bytes 1179652
  4.3 0.9 %copy-start.6 = (s32[4,64,128]{2,1,0:T(8,128)S(1)}, s32[4,64,128]{2,1,0:T(8,128)}, u32[]{:S(2)}) copy-start(s32[4,64,128]{2,1,0:T(8,128)} %refs_7_.1) | copy-start | bytes 393220
  5.2 0.8 copy-start.8
  6.0 0.7 copy-start.11
  6.6 27.2 %copy-start.1 = (bf16[2,3,4,64,128]{4,3,2,1,0:T(8,128)(2,1)S(1)}, bf16[2,3,4,64,128]{4,3,2,1,0:T(8,128)(2,1)}, u32[]{:S(2)}) copy-start(bf16[2,3,4,64,128]{4,3,2,1,0:T(8,128)(2,1)} %refs_6_.1) | copy-start | bytes 1179652
  6.7 27.2 %copy-start.3 = (f32[3,4,64,128]{3,2,1,0:T(8,128)S(1)}, f32[3,4,64,128]{3,2,1,0:T(8,128)}, u32[]{:S(2)}) copy-start(f32[3,4,64,128]{3,2,1,0:T(8,128)} %refs_0_.1) | copy-start | bytes 1179652
  6.7 27.2 %copy-start.5 = (f32[3,4,64,128]{3,2,1,0:T(8,128)S(1)}, f32[3,4,64,128]{3,2,1,0:T(8,128)}, u32[]{:S(2)}) copy-start(f32[3,4,64,128]{3,2,1,0:T(8,128)} %refs_1_.1) | copy-start | bytes 1179652
  8.2 25.7 %copy-start.7 = (s32[4,64,128]{2,1,0:T(8,128)S(1)}, s32[4,64,128]{2,1,0:T(8,128)}, u32[]{:S(2)}) copy-start(s32[4,64,128]{2,1,0:T(8,128)} %refs_7_.1) | copy-start | bytes 393220
  8.2 25.7 %all-to-all-start = ((f32[256,1,128]{2,1,0:T(1,128)}), f32[256,1,128]{2,1,0:T(1,128)S(1)}, u32[]{:S(2)}, u32[]{:S(2)}) async-start(f32[256,1,128]{2,1,0:T(1,128)} %get-tuple-element.27), calls=%async_computation | async-start | bytes 262144 | tf_op jit(solution)/shard_map/all_to_all | solution.py:415
  22.9 3.8 %collective-permute-start = (f32[58,8,128]{2,1,0:T(8,128)S(1)}, f32[58,8,128]{2,1,0:T(8,128)S(1)}, u32[]{:S(2)}, u32[]{:S(2)}) collective-permute-start(f32[58,8,128]{2,1,0:T(8,128)S(1)} %get-tuple-element.25), channel_id=1, source_target_pairs={{0,8},{8,0},{16,24},{24,16},{32,40},{40,32},{48,56},{56,48},{64,72... | collective-permute-start | bytes 712712 | tf_op jit(solution)/shard_map/ppermute | solution.py:24
  23.4 10.5 %copy-start.12 = (f32[4]{0:T(128)S(1)}, f32[4]{0:T(128)}, u32[]{:S(2)}) copy-start(f32[4]{0:T(128)} %refs_13_.1) | copy-start | bytes 52
  23.4 10.6 %copy-start.13 = (f32[4]{0:T(128)S(1)}, f32[4]{0:T(128)}, u32[]{:S(2)}) copy-start(f32[4]{0:T(128)} %refs_14_.1) | copy-start | bytes 52
  23.4 10.1 %collective-permute-start.1 = (f32[58,8,128]{2,1,0:T(8,128)S(1)}, f32[58,8,128]{2,1,0:T(8,128)S(1)}, u32[]{:S(2)}, u32[]{:S(2)}) collective-permute-start(f32[58,8,128]{2,1,0:T(8,128)S(1)} %get-tuple-element.26), channel_id=1, source_target_pairs={{8,16},{16,8},{24,32},{32,24},{40,48},{48,40},{56,64},{64,56},{72,... | collective-permute-start | bytes 712712 | tf_op jit(solution)/shard_map/ppermute | solution.py:30
  33.9 7.3 %copy-start.9 = (f32[64,128]{1,0:T(8,128)S(1)}, f32[64,128]{1,0:T(8,128)}, u32[]{:S(2)}) copy-start(f32[64,128]{1,0:T(8,128)} %density.3) | copy-start | bytes 98308
  35.2 7.3 %collective-permute-start.2 = (f32[144,128]{1,0:T(8,128)S(1)}, f32[144,128]{1,0:T(8,128)S(1)}, u32[]{:S(2)}, u32[]{:S(2)}) collective-permute-start(f32[144,128]{1,0:T(8,128)S(1)} %get-tuple-element.33), channel_id=1, source_target_pairs={{0,1},{1,0},{2,3},{3,2},{4,5},{5,4},{6,7},{7,6},{8,9},{9,8},{10,11... | collective-permute-start | bytes 221192 | tf_op jit(solution)/shard_map/ppermute | solution.py:24
  40.6 1.9 %collective-permute-start.3 = (f32[144,128]{1,0:T(8,128)S(1)}, f32[144,128]{1,0:T(8,128)S(1)}, u32[]{:S(2)}, u32[]{:S(2)}) collective-permute-start(f32[144,128]{1,0:T(8,128)S(1)} %get-tuple-element.34), channel_id=1, source_target_pairs={{1,2},{2,1},{3,4},{4,3},{5,6},{6,5},{9,10},{10,9},{11,12},{12,11},... | collective-permute-start | bytes 221192 | tf_op jit(solution)/shard_map/ppermute | solution.py:30
  43.6 10.6 %collective-permute-start.4 = (f32[208,128]{1,0:T(8,128)S(1)}, f32[208,128]{1,0:T(8,128)S(1)}, u32[]{:S(2)}, u32[]{:S(2)}) collective-permute-start(f32[208,128]{1,0:T(8,128)S(1)} %get-tuple-element.38.mine), channel_id=1, source_target_pairs={{0,1},{1,0},{2,3},{3,2},{4,5},{5,4},{6,7},{7,6},{8,9},{9,8},{10,11... | collective-permute-start | bytes 319496 | tf_op jit(solution)/shard_map/ppermute | solution.py:24
  54.9 15.7 %all-to-all-start.1 = ((f32[4,64,128]{2,1,0:T(8,128)}), f32[4,64,128]{2,1,0:T(8,128)S(1)}, u32[]{:S(2)}, u32[]{:S(2)}) async-start(f32[4,64,128]{2,1,0:T(8,128)} %pair.1), calls=%async_computation.1 | async-start | bytes 262144 | tf_op jit(solution)/shard_map/all_to_all | solution.py:443
  65.8 9.9 %collective-permute-start.5 = (f32[144,128]{1,0:T(8,128)S(1)}, f32[144,128]{1,0:T(8,128)S(1)}, u32[]{:S(2)}, u32[]{:S(2)}) collective-permute-start(f32[144,128]{1,0:T(8,128)S(1)} %get-tuple-element.39), channel_id=1, source_target_pairs={{1,2},{2,1},{3,4},{4,3},{5,6},{6,5},{9,10},{10,9},{11,12},{12,11},... | collective-permute-start | bytes 221192 | tf_op jit(solution)/shard_map/ppermute | solution.py:30
  70.6 6.1 %collective-permute-start.6 = (f32[16,128]{1,0:T(8,128)S(1)}, f32[16,128]{1,0:T(8,128)S(1)}, u32[]{:S(2)}, u32[]{:S(2)}) collective-permute-start(f32[16,128]{1,0:T(8,128)S(1)} %get-tuple-element.43), channel_id=1, source_target_pairs={{0,8},{8,0},{16,24},{24,16},{32,40},{40,32},{48,56},{56,48},{64,72... | collective-permute-start | bytes 24584 | tf_op jit(solution)/shard_map/ppermute | solution.py:24
  73.0 7.1 %collective-permute-start.7 = (f32[16,128]{1,0:T(8,128)S(1)}, f32[16,128]{1,0:T(8,128)S(1)}, u32[]{:S(2)}, u32[]{:S(2)}) collective-permute-start(f32[16,128]{1,0:T(8,128)S(1)} %get-tuple-element.44), channel_id=1, source_target_pairs={{8,16},{16,8},{24,32},{32,24},{40,48},{48,40},{56,64},{64,56},{72,... | collective-permute-start | bytes 24584 | tf_op jit(solution)/shard_map/ppermute | solution.py:30
